TPU v7x, 32 devices: a whole 2x2x4 slice. The times are simulated.
32 devices in a mesh: delay: 4 (over z), row: 4 (over x, core), col: 2 (over y).
Axes of the slice: x: 2, y: 2, z: 4, core: 2. Of those that a mesh axis runs over, the one named last changes fastest.
Arguments:
- operators: float32 [4, 9216, 9216], P('delay', 'col', 'row'), may hold values from -0.0625 to 0.0625
- excitation: float32 [3, 9216, 256], P(None, 'col'), may hold values from -6 to 6
- pending: float32 [4, 9216, 256], P('delay', 'col', 'row'), may hold values from -6 to 6
- sheet_gain: float32 [9216], P('row'), may hold values from 0.2 to 2
Outputs:
- currents: float32 [3, 9216, 256], P(None, 'row', 'col')
- remaining: float32 [4, 9216, 256], P('delay', 'col', 'row')
All inputs are finite; a program needn't handle non-finite values.
Results may differ from a plain program's by a relative error of at most 0.00014.
Values sent between devices are 32-bit elements; how exact they have to be, the bound alone decides.
A program may use at most 128 MiB of HBM per device.

v0:
```python
import jax
import jax.numpy as jnp
from jax import lax
from jax.sharding import PartitionSpec as P

STEPS = 3


def spread(block, axis, source):
    block = jnp.where(lax.axis_index(axis) == source, block, jnp.zeros_like(block))
    return lax.psum(block, axis)


def passed_along(value, axis, steps):
    count = lax.axis_size(axis)
    initial, last = (max(0, -steps), min(count, count - steps))
    return lax.ppermute(value, axis, [(source, source + steps) for source in range(initial, last)])


def local(operators, excitation, pending, sheet_gain):
    local_block = operators[0]
    is_head = lax.axis_index("delay") == 0
    future = pending[0]

    def admit_apply(driving):
        return lax.dot_general(
            local_block,
            driving,
            (((0,), (0,)), ((), ())),
            precision=lax.Precision.HIGHEST,
            preferred_element_type=jnp.float32,
        )

    def admit_skip(driving):
        return jnp.zeros((local_block.shape[1], driving.shape[1]), jnp.float32)

    def radiate_apply(source_piece):
        return jnp.dot(
            local_block,
            source_piece,
            precision=lax.Precision.HIGHEST,
            preferred_element_type=jnp.float32,
        )

    def radiate_skip(source_piece):
        return jnp.zeros((local_block.shape[0], source_piece.shape[1]), jnp.float32)

    outputs = []
    for moment in range(STEPS):
        due_field = lax.all_gather(future, "row", axis=1, tiled=True)
        driving = excitation[moment] - due_field
        partial_value = lax.cond(is_head, admit_apply, admit_skip, driving)
        sheet_current = lax.psum_scatter(partial_value, "col", scatter_dimension=1, tiled=True)
        current = sheet_current / (1.0 + sheet_gain[:, None] * sheet_current * sheet_current)
        current = spread(current, "delay", 0)
        outputs.append(current)
        field_part = lax.cond(
            is_head, radiate_skip, radiate_apply, lax.all_gather(current, "col", axis=1, tiled=True)
        )
        summed = future + lax.psum_scatter(field_part, "row", scatter_dimension=1, tiled=True)
        future = passed_along(summed, "delay", -1)
    return (jnp.stack(outputs), future[None])


def solution(mesh):
    in_specs = (P("delay", "col", "row"), P(None, "col", None), P("delay", "col", "row"), P("row"))
    out_specs = (P(None, "row", "col"), P("delay", "col", "row"))
    return jax.shard_map(local, mesh=mesh, in_specs=in_specs, out_specs=out_specs, check_vma=False)
```

profile of v0, /device:TPU:16, one launch (start us, length us, event | category | flops | bytes accessed | tf_op | source)
XLA Modules:
  0.0 1040.2 jit_solution(828634252288957588)
XLA Ops:
  7.2 3.5 copy.15
  10.8 38.6 %all-gather.18.cloned.1.call-done = f32[1,4608,256]{1,0,2:T(1,128)} async-done(((f32[1,4608,64]{1,0,2:T(1,128)}), f32[1,4608,256]{1,0,2:T(1,128)}) %all-gather.18.cloned.1.call-update) | async-done | bytes 4718608 | tf_op jit(solution)/shard_map/all_gather | solution.py:50
  49.4 4.8 copy.27
  56.4 78.7 %reduce-scatter.7.cloned.1.call-done = f32[2304,128]{1,0:T(8,128)} async-done(((f32[2304,256]{1,0:T(8,128)}), f32[2304,128]{1,0:T(8,128)}) %reduce-scatter.7.cloned.1.call-update) | async-done | bytes 1179664 | tf_op jit(solution)/shard_map/reduce_scatter | solution.py:53
  135.0 2.7 fusion.11
  137.8 55.7 %all-reduce.4.cloned.1.call-done = f32[2304,128]{1,0:T(8,128)} async-done(((f32[2304,128]{1,0:T(8,128)}), f32[2304,128]{1,0:T(8,128)}) %all-reduce.4.cloned.1.call-update) | async-done | bytes 1179664 | tf_op jit(solution)/shard_map/psum | solution.py:11
  193.5 37.4 %all-gather.8.cloned.1.call-done = f32[2304,256]{1,0:T(8,128)} async-done(((f32[2304,128]{1,0:T(8,128)}), f32[2304,256]{1,0:T(8,128)}) %all-gather.8.cloned.1.call-update) | async-done | bytes 2359312 | tf_op jit(solution)/shard_map/all_gather | solution.py:58
  230.9 38.9 %conditional.7 = (f32[4608,256]{1,0:T(8,128)}) conditional(s32[]{:T(128)} %convert_element_type.2, (f32[4608,2304]{1,0:T(8,128)}, f32[2304,256]{1,0:T(8,128)}) %tuple.107, () %tuple.48), branch_computations={%region_4.5_spmd, %region_5.6_spmd} | conditional | flops 32614907904 | bytes 49545224 | solution.py:57
  231.0 38.7 %fusion.18 = f32[4608,256]{1,0:T(8,128)} fusion(f32[4608,2304]{1,0:T(8,128)} %get-tuple-element.60, f32[2304,256]{1,0:T(8,128)} %get-tuple-element.61), kind=kOutput, calls=%fused_computation.27 | convolution fusion | flops 32614907904 | bytes 49545216 | tf_op jit(solution)/shard_map/cond/branch_0_fun/dot_general | solution.py:38
  269.7 6.1 copy.18
  275.9 48.1 %reduce-scatter.9.cloned.1.call-done = f32[4608,64]{0,1:T(8,128)} async-done(((f32[4608,256]{0,1:T(8,128)}), f32[4608,64]{0,1:T(8,128)}) %reduce-scatter.9.cloned.1.call-update) | async-done | bytes 1179664 | tf_op jit(solution)/shard_map/reduce_scatter | solution.py:60
  327.8 27.0 %collective-permute-done = f32[4608,64]{0,1:T(8,128)S(1)} collective-permute-done((f32[4608,64]{0,1:T(8,128)S(1)}, f32[4608,64]{0,1:T(8,128)S(1)}, u32[]{:S(2)}, u32[]{:S(2)}) %collective-permute-start) | collective-permute-done | bytes 1179680 | tf_op jit(solution)/shard_map/ppermute | solution.py:17
  355.9 36.6 %all-gather.10.cloned.1.call-done = f32[4608,256]{0,1:T(8,128)} async-done(((f32[4608,64]{0,1:T(8,128)}), f32[4608,256]{0,1:T(8,128)}) %all-gather.10.cloned.1.call-update) | async-done | bytes 4718608 | tf_op jit(solution)/shard_map/all_gather | solution.py:50
  395.0 78.7 %reduce-scatter.11.cloned.1.call-done = f32[2304,128]{1,0:T(8,128)} async-done(((f32[2304,256]{1,0:T(8,128)}), f32[2304,128]{1,0:T(8,128)}) %reduce-scatter.11.cloned.1.call-update) | async-done | bytes 1179664 | tf_op jit(solution)/shard_map/reduce_scatter | solution.py:53
  473.6 2.7 fusion.14
  476.4 55.7 %all-reduce.6.cloned.1.call-done = f32[2304,128]{1,0:T(8,128)} async-done(((f32[2304,128]{1,0:T(8,128)}), f32[2304,128]{1,0:T(8,128)}) %all-reduce.6.cloned.1.call-update) | async-done | bytes 1179664 | tf_op jit(solution)/shard_map/psum | solution.py:11
  532.1 37.5 %all-gather.12.cloned.1.call-done = f32[2304,256]{1,0:T(8,128)} async-done(((f32[2304,128]{1,0:T(8,128)}), f32[2304,256]{1,0:T(8,128)}) %all-gather.12.cloned.1.call-update) | async-done | bytes 2359312 | tf_op jit(solution)/shard_map/all_gather | solution.py:58
  569.6 39.2 %conditional.9 = (f32[4608,256]{1,0:T(8,128)}) conditional(s32[]{:T(128)} %convert_element_type.2, (f32[4608,2304]{1,0:T(8,128)}, f32[2304,256]{1,0:T(8,128)}) %tuple.109, () %tuple.52), branch_computations={%region_11.12_spmd, %region_12.13_spmd} | conditional | flops 32614907904 | bytes 49545224 | solution.py:57
  570.0 38.7 %fusion.19 = f32[4608,256]{1,0:T(8,128)} fusion(f32[4608,2304]{1,0:T(8,128)} %get-tuple-element.65, f32[2304,256]{1,0:T(8,128)} %get-tuple-element.66), kind=kOutput, calls=%fused_computation.28 | convolution fusion | flops 32614907904 | bytes 49545216 | tf_op jit(solution)/shard_map/cond/branch_0_fun/dot_general | solution.py:38
  608.7 6.1 copy.21
  614.9 48.1 %reduce-scatter.13.cloned.1.call-done = f32[4608,64]{0,1:T(8,128)} async-done(((f32[4608,256]{0,1:T(8,128)}), f32[4608,64]{0,1:T(8,128)}) %reduce-scatter.13.cloned.1.call-update) | async-done | bytes 1179664 | tf_op jit(solution)/shard_map/reduce_scatter | solution.py:60
  666.8 27.0 %collective-permute-done.1 = f32[4608,64]{0,1:T(8,128)S(1)} collective-permute-done((f32[4608,64]{0,1:T(8,128)S(1)}, f32[4608,64]{0,1:T(8,128)S(1)}, u32[]{:S(2)}, u32[]{:S(2)}) %collective-permute-start.1) | collective-permute-done | bytes 1179680 | tf_op jit(solution)/shard_map/ppermute | solution.py:17
  694.9 36.6 %all-gather.14.cloned.1.call-done = f32[4608,256]{0,1:T(8,128)} async-done(((f32[4608,64]{0,1:T(8,128)}), f32[4608,256]{0,1:T(8,128)}) %all-gather.14.cloned.1.call-update) | async-done | bytes 4718608 | tf_op jit(solution)/shard_map/all_gather | solution.py:50
  733.9 78.7 %reduce-scatter.15.cloned.1.call-done = f32[2304,128]{1,0:T(8,128)} async-done(((f32[2304,256]{1,0:T(8,128)}), f32[2304,128]{1,0:T(8,128)}) %reduce-scatter.15.cloned.1.call-update) | async-done | bytes 1179664 | tf_op jit(solution)/shard_map/reduce_scatter | solution.py:53
  812.5 2.7 fusion.17
  815.3 55.7 %all-reduce.8.cloned.1.call-done = f32[2304,128]{1,0:T(8,128)} async-done(((f32[2304,128]{1,0:T(8,128)}), f32[2304,128]{1,0:T(8,128)}) %all-reduce.8.cloned.1.call-update) | async-done | bytes 1179664 | tf_op jit(solution)/shard_map/psum | solution.py:11
  871.0 37.4 %all-gather.16.cloned.1.call-done = f32[2304,256]{1,0:T(8,128)} async-done(((f32[2304,128]{1,0:T(8,128)}), f32[2304,256]{1,0:T(8,128)}) %all-gather.16.cloned.1.call-update) | async-done | bytes 2359312 | tf_op jit(solution)/shard_map/all_gather | solution.py:58
  908.4 38.9 %conditional.11 = (f32[4608,256]{1,0:T(8,128)}) conditional(s32[]{:T(128)} %convert_element_type.2, (f32[4608,2304]{1,0:T(8,128)}, f32[2304,256]{1,0:T(8,128)}) %tuple.111, () %tuple.55), branch_computations={%region_18.19_spmd, %region_19.20_spmd} | conditional | flops 32614907904 | bytes 49545224 | solution.py:57
  908.6 38.7 %fusion.20 = f32[4608,256]{1,0:T(8,128)} fusion(f32[4608,2304]{1,0:T(8,128)} %get-tuple-element.70, f32[2304,256]{1,0:T(8,128)} %get-tuple-element.71), kind=kOutput, calls=%fused_computation.29 | convolution fusion | flops 32614907904 | bytes 49545216 | tf_op jit(solution)/shard_map/cond/branch_0_fun/dot_general | solution.py:38
  947.2 6.1 copy.24
  953.4 48.1 %reduce-scatter.17.cloned.1.call-done = f32[4608,64]{0,1:T(8,128)} async-done(((f32[4608,256]{0,1:T(8,128)}), f32[4608,64]{0,1:T(8,128)}) %reduce-scatter.17.cloned.1.call-update) | async-done | bytes 1179664 | tf_op jit(solution)/shard_map/reduce_scatter | solution.py:60
  1007.6 24.8 %collective-permute-done.2 = f32[4608,64]{0,1:T(8,128)S(1)} collective-permute-done((f32[4608,64]{0,1:T(8,128)S(1)}, f32[4608,64]{0,1:T(8,128)S(1)}, u32[]{:S(2)}, u32[]{:S(2)}) %collective-permute-start.2) | collective-permute-done | bytes 1179680 | tf_op jit(solution)/shard_map/ppermute | solution.py:17
  (65 shorter events, 24.9 us)
Async XLA Ops:
  7.2 42.2 %all-gather.18.cloned.1.call-start = ((), (), s32[]{:S(2)}) async-start(), calls=%async_computation.20 | async-start | bytes 5898240 | tf_op jit(solution)/shard_map/all_gather | solution.py:50
  10.7 124.3 %reduce-scatter.7.cloned.1.call-start = ((), (), s32[]{:S(2)}) async-start(), calls=%async_computation.6 | async-start | bytes 3538944 | tf_op jit(solution)/shard_map/reduce_scatter | solution.py:53
  56.3 78.8 %copy-start.8 = (f32[2304]{0:T(1024)S(1)}, f32[2304]{0:T(1024)}, u32[]{:S(2)}) copy-start(f32[2304]{0:T(1024)} %param.19) | copy-start | bytes 27652
  56.3 137.1 %all-reduce.4.cloned.1.call-start = ((), (), s32[]{:S(2)}) async-start(), calls=%async_computation.7 | async-start | bytes 2359296 | tf_op jit(solution)/shard_map/psum | solution.py:11
  137.7 93.1 %all-gather.8.cloned.1.call-start = ((), (), s32[]{:S(2)}) async-start(), calls=%async_computation.8 | async-start | bytes 3538944 | tf_op jit(solution)/shard_map/all_gather | solution.py:58
  193.5 130.5 %reduce-scatter.9.cloned.1.call-start = ((), (), s32[]{:S(2)}) async-start(), calls=%async_computation.9 | async-start | bytes 5898240 | tf_op jit(solution)/shard_map/reduce_scatter | solution.py:60
  275.8 48.2 %copy-start = (f32[1,4608,64]{1,2,0:T(8,128)S(1)}, f32[1,4608,64]{1,2,0:T(8,128)}, u32[]{:S(2)}) copy-start(f32[1,4608,64]{1,2,0:T(8,128)} %param.18) | copy-start | bytes 3538948
  275.8 116.7 %all-gather.10.cloned.1.call-start = ((), (), s32[]{:S(2)}) async-start(), calls=%async_computation.10 | async-start | bytes 5898240 | tf_op jit(solution)/shard_map/all_gather | solution.py:50
  325.4 29.4 %collective-permute-start = (f32[4608,64]{0,1:T(8,128)S(1)}, f32[4608,64]{0,1:T(8,128)S(1)}, u32[]{:S(2)}, u32[]{:S(2)}) collective-permute-start(f32[4608,64]{0,1:T(8,128)S(1)} %bitcast_add_fusion), channel_id=1, source_target_pairs={{8,0},{16,8},{24,16},{9,1},{17,9},{25,17},{10,2},{18,10},{26,18},{... | collective-permute-start | bytes 3538952 | tf_op jit(solution)/shard_map/ppermute | solution.py:17
  354.8 1.0 copy-start.3
  355.8 117.8 %reduce-scatter.11.cloned.1.call-start = ((), (), s32[]{:S(2)}) async-start(), calls=%async_computation.11 | async-start | bytes 3538944 | tf_op jit(solution)/shard_map/reduce_scatter | solution.py:53
  394.9 137.1 %all-reduce.6.cloned.1.call-start = ((), (), s32[]{:S(2)}) async-start(), calls=%async_computation.12 | async-start | bytes 2359296 | tf_op jit(solution)/shard_map/psum | solution.py:11
  476.3 93.3 %all-gather.12.cloned.1.call-start = ((), (), s32[]{:S(2)}) async-start(), calls=%async_computation.13 | async-start | bytes 3538944 | tf_op jit(solution)/shard_map/all_gather | solution.py:58
  532.0 130.9 %reduce-scatter.13.cloned.1.call-start = ((), (), s32[]{:S(2)}) async-start(), calls=%async_computation.14 | async-start | bytes 5898240 | tf_op jit(solution)/shard_map/reduce_scatter | solution.py:60
  614.8 48.2 %copy-start.4 = (f32[4608,64]{0,1:T(8,128)S(1)}, f32[4608,64]{0,1:T(8,128)}, u32[]{:S(2)}) copy-start(f32[4608,64]{0,1:T(8,128)} %copy-done.3) | copy-start | bytes 3538948
  614.8 116.7 %all-gather.14.cloned.1.call-start = ((), (), s32[]{:S(2)}) async-start(), calls=%async_computation.15 | async-start | bytes 5898240 | tf_op jit(solution)/shard_map/all_gather | solution.py:50
  664.4 29.4 %collective-permute-start.1 = (f32[4608,64]{0,1:T(8,128)S(1)}, f32[4608,64]{0,1:T(8,128)S(1)}, u32[]{:S(2)}, u32[]{:S(2)}) collective-permute-start(f32[4608,64]{0,1:T(8,128)S(1)} %add.39), channel_id=1, source_target_pairs={{8,0},{16,8},{24,16},{9,1},{17,9},{25,17},{10,2},{18,10},{26,18},{... | collective-permute-start | bytes 3538952 | tf_op jit(solution)/shard_map/ppermute | solution.py:17
  693.8 1.0 copy-start.5
  694.8 117.7 %reduce-scatter.15.cloned.1.call-start = ((), (), s32[]{:S(2)}) async-start(), calls=%async_computation.16 | async-start | bytes 3538944 | tf_op jit(solution)/shard_map/reduce_scatter | solution.py:53
  733.8 137.1 %all-reduce.8.cloned.1.call-start = ((), (), s32[]{:S(2)}) async-start(), calls=%async_computation.17 | async-start | bytes 2359296 | tf_op jit(solution)/shard_map/psum | solution.py:11
  815.2 93.2 %all-gather.16.cloned.1.call-start = ((), (), s32[]{:S(2)}) async-start(), calls=%async_computation.18 | async-start | bytes 3538944 | tf_op jit(solution)/shard_map/all_gather | solution.py:58
  871.0 130.5 %reduce-scatter.17.cloned.1.call-start = ((), (), s32[]{:S(2)}) async-start(), calls=%async_computation.19 | async-start | bytes 5898240 | tf_op jit(solution)/shard_map/reduce_scatter | solution.py:60
  953.3 48.2 %copy-start.6 = (f32[4608,64]{0,1:T(8,128)S(1)}, f32[4608,64]{0,1:T(8,128)}, u32[]{:S(2)}) copy-start(f32[4608,64]{0,1:T(8,128)} %copy-done.5) | copy-start | bytes 3538948
  953.3 52.1 %copy-start.1 = (f32[2304,128]{1,0:T(8,128)S(1)}, f32[2304,128]{1,0:T(8,128)}, u32[]{:S(2)}) copy-start(f32[2304,128]{1,0:T(8,128)} %all-reduce.4.cloned.1.call-done) | copy-start | bytes 3538948
  953.4 52.1 %copy-start.2 = (f32[2304,128]{1,0:T(8,128)S(1)}, f32[2304,128]{1,0:T(8,128)}, u32[]{:S(2)}) copy-start(f32[2304,128]{1,0:T(8,128)} %all-reduce.6.cloned.1.call-done) | copy-start | bytes 3538948
  1001.5 4.0 copy-start.7
  1003.0 29.4 %collective-permute-start.2 = (f32[4608,64]{0,1:T(8,128)S(1)}, f32[4608,64]{0,1:T(8,128)S(1)}, u32[]{:S(2)}, u32[]{:S(2)}) collective-permute-start(f32[4608,64]{0,1:T(8,128)S(1)} %add.41), channel_id=1, source_target_pairs={{8,0},{16,8},{24,16},{9,1},{17,9},{25,17},{10,2},{18,10},{26,18},{... | collective-permute-start | bytes 3538952 | tf_op jit(solution)/shard_map/ppermute | solution.py:17
Sparse Core Ops, SparseCore 0:
  10.9 38.4 all-gather.17
  56.4 78.5 reduce-scatter.6
  138.0 55.3 all-reduce.3
  194.8 35.9 all-gather.7
  276.0 47.9 reduce-scatter.8
  356.0 36.5 all-gather.9
  395.3 78.2 reduce-scatter.10
  476.6 55.3 all-reduce.5
  533.6 35.9 all-gather.11
  615.0 47.9 reduce-scatter.12
  694.9 36.5 all-gather.13
  734.2 78.3 reduce-scatter.14
  815.5 55.4 all-reduce.7
  872.3 35.9 all-gather.15
  953.5 47.9 reduce-scatter.16
where the time goes:
time: 1050 us; the launch traced here: 1040 us
  waiting for transfers between devices  850 us (81%)
  matrix products  116 us (11%)
  local copies, waits for them, and re-layouts  35.9 us (3%)
  other arithmetic  14.4 us (1%)
  between operations  14.3 us (1%)
    reduce_scatter x3, waiting for transfers between devices, local(): lax.psum_scatter(partial_value, 'col', scatter_dimension=1, tiled=True)  236 us
    psum x3, waiting for transfers between devices, spread(): return lax.psum(block, axis)  167 us
    reduce_scatter x3, waiting for transfers between devices, local(): lax.psum_scatter(field_part, 'row', scatter_dimension=1, tiled=True)  144 us
    dot_general x3, matrix products, radiate_apply(): jnp.dot(local_block, source_piece, precision=lax.Precision.HIGHEST, prefe...  116 us
    all_gather x3, waiting for transfers between devices, local(): lax.all_gather(current, 'col', axis=1, tiled=True)  112 us
    all_gather x3, waiting for transfers between devices, local(): due_field = lax.all_gather(future, 'row', axis=1, tiled=True)  112 us
    ppermute x3, waiting for transfers between devices, passed_along(): lax.ppermute(value, axis, [(source, source + steps) for source in range(i...  78.7 us
  transfers between devices with their start and end apart: 18, of which 18 were waited for; matrix products, arithmetic and copies ran while one was open for 0% of the time, Pallas kernels for 0%

commit v1 on v0

v1 whole, which is shorter than its diff:
```python
import jax
import jax.numpy as jnp
from jax import lax
from jax.sharding import PartitionSpec as P

STEPS = 3
CHUNKS = 2
SKEW = 1
AXES = ("delay", "row", "col")


def local(operators, excitation, pending, sheet_gain):
    block = operators[0]
    groups, rows, cols = (lax.axis_size(a) for a in AXES)
    d, r, c = (lax.axis_index(a) for a in AXES)
    is_head = d == 0
    tests, basis = block.shape
    finest = max(rows, cols)
    width = excitation.shape[2] // (finest * CHUNKS)
    stages = STEPS * CHUNKS
    slots = stages + SKEW * (groups - 1)

    def place(dd, rr, cc):
        return (dd * rows + rr) * cols + cc

    def active(s):
        return [dd for dd in range(groups) if 0 <= s - SKEW * dd < stages]

    def exchange(x, axis, bit, members):
        pairs = []
        for dd in members:
            for rr in range(rows):
                for cc in range(cols):
                    to = (dd, rr ^ bit, cc) if axis == "row" else (dd, rr, cc ^ bit)
                    pairs.append((place(dd, rr, cc), place(*to)))
        return lax.ppermute(x, AXES, pairs)

    def shift(x, step, members):
        pairs = [
            (place(dd, rr, cc), place(dd + step, rr, cc))
            for dd in members
            if 0 <= dd + step < groups
            for rr in range(rows)
            for cc in range(cols)
        ]
        return lax.ppermute(x, AXES, pairs) if pairs else jnp.zeros_like(x)

    def scatter_sum(x, axis, members):
        n = lax.axis_size(axis)
        at = r if axis == "row" else c
        w = x.shape[0] // n
        x = x.reshape(n, w, -1)
        bit = 1
        while bit < n:
            x = x.reshape(x.shape[0] // 2, 2, w, -1)
            mine = (at // bit) % 2
            kept = lax.dynamic_index_in_dim(x, mine, 1, keepdims=False)
            other = lax.dynamic_index_in_dim(x, 1 - mine, 1, keepdims=False)
            x = kept + exchange(other, axis, bit, members)
            bit *= 2
        return x[0]

    def gather(x, axis, members):
        n = lax.axis_size(axis)
        at = r if axis == "row" else c
        w, length = x.shape
        x = x[None]
        bit = n // 2
        while bit:
            got = exchange(x, axis, bit, members)
            mine = (at // bit) % 2
            low = jnp.where(mine == 0, x, got)
            high = jnp.where(mine == 0, got, x)
            x = jnp.stack([low, high], axis=1).reshape(-1, w, length)
            bit //= 2
        return x.reshape(n * w, length)

    def product(a, dims):
        return lax.dot_general(
            a, block, (dims, ((), ())), precision=lax.Precision.HIGH, preferred_element_type=jnp.float32
        )

    driven = excitation.transpose(0, 2, 1).reshape(STEPS, finest, CHUNKS, width, tests)
    driven = lax.optimization_barrier(driven.transpose(0, 2, 1, 3, 4))
    waiting = pending[0].T.reshape(finest // rows, CHUNKS, width, tests)
    gain = sheet_gain[None, :]
    held, updated, arrived = [], [], {}

    def future_at(s):
        stage = s - SKEW * d
        source = s - CHUNKS + SKEW
        got = shift(updated[source], -1, [dd for dd in active(source) if dd > 0]) if source >= 0 else None
        arrived[s] = got
        if s >= CHUNKS + SKEW * (groups - 1):
            return got
        first = lax.dynamic_index_in_dim(waiting, jnp.clip(stage, 0, CHUNKS - 1), 1, keepdims=False)
        first = first.reshape(-1, tests)
        return first if got is None else jnp.where(stage < CHUNKS, first, got)

    for s in range(slots):
        members = active(s)
        tail = [dd for dd in members if dd > 0]
        future = future_at(s)
        current = shift(held[s - SKEW], 1, active(s - SKEW)) if s >= SKEW else None
        driving = whole = None
        if 0 in members:
            driving = gather(future, "row", [0])
        if tail:
            whole = gather(current, "col", tail)
        driving, whole, future, current = lax.optimization_barrier((driving, whole, future, current))
        fresh, new = current, future
        if driving is not None:
            driving = driven[s // CHUNKS, s % CHUNKS].reshape(-1, tests) - driving
            part = lax.cond(
                is_head,
                lambda x: product(x, ((1,), (0,))),
                lambda x: jnp.zeros((x.shape[0], basis), jnp.float32),
                driving,
            )
        if whole is not None:
            field = lax.cond(
                is_head,
                lambda x: jnp.zeros((x.shape[0], tests), jnp.float32),
                lambda x: product(x, ((1,), (1,))),
                whole,
            )
        if driving is not None:
            sheet = scatter_sum(part, "col", [0])
            fresh = sheet / (1.0 + gain * sheet * sheet)
            if current is not None:
                fresh = jnp.where(is_head, fresh, current)
        if whole is not None:
            new = future + scatter_sum(field, "row", tail)
        fresh, new = lax.optimization_barrier((fresh, new))
        held.append(fresh)
        updated.append(new)

    for s in range(slots, stages + CHUNKS + SKEW * (groups - 2)):
        future_at(s)

    def outputs_of(dd):
        def build(held, got):
            mine = held[SKEW * dd : SKEW * dd + stages]
            now = jnp.stack(mine).reshape(STEPS, CHUNKS, finest // cols, width, basis)
            now = now.transpose(0, 4, 2, 1, 3).reshape(STEPS, basis, -1)
            if dd == groups - 1:
                return now, jnp.zeros((1, tests, pending.shape[2]), jnp.float32)
            last = [got[stages + SKEW * dd + i - stages] for i in range(CHUNKS)]
            last = jnp.stack(last).reshape(CHUNKS, finest // rows, width, tests)
            return now, last.transpose(3, 1, 0, 2).reshape(1, tests, -1)

        return build

    got = [arrived[s] for s in range(stages, stages + CHUNKS + SKEW * (groups - 2))]
    return lax.switch(d, [outputs_of(dd) for dd in range(groups)], held, got)


def solution(mesh):
    in_specs = (P("delay", "col", "row"), P(None, "col", None), P("delay", "col", "row"), P("row"))
    out_specs = (P(None, "row", "col"), P("delay", "col", "row"))
    return jax.shard_map(local, mesh=mesh, in_specs=in_specs, out_specs=out_specs, check_vma=False)
```

time: 1050 us -> 825 us (0.79)
  waiting for transfers between devices: 850 us -> 424 us
  matrix products: 116 us -> 215 us
  starting transfers between devices: 7.96 us -> 105 us
  between operations: 14.3 us -> 2.49 us
  local copies, waits for them, and re-layouts: 35.9 us -> 46.9 us
    reduce_scatter x6 -> x0, waiting for transfers between devices: 380 us -> none  [the longest x3 236 us: local(): lax.psum_scatter(partial_value, 'col', scatter_dimension=1, tiled=True)]
    ppermute x3 -> x58, waiting for transfers between devices: 78.7 us -> 424 us  [the longest x16 267 us: shift(): return lax.ppermute(x, AXES, pairs) if pairs else jnp.zeros_like(x)]
    all_gather x6 -> x0, waiting for transfers between devices: 224 us -> none  [the longest x3 112 us: local(): lax.all_gather(current, 'col', axis=1, tiled=True)]
    psum x3 -> x0, waiting for transfers between devices: 167 us -> none  [spread(): return lax.psum(block, axis)]
    dot_general x3 -> x8, matrix products: 116 us -> 215 us  [product(): lax.dot_general(a, block, (dims, ((), ())), precision=lax.Precision.HIGH,...]
    ppermute x3 -> x58, starting transfers between devices: 7.35 us -> 105 us  [the longest x42 66.6 us: exchange(): return lax.ppermute(x, AXES, pairs)]
    cond x6 -> x8, local copies, waits for them, and re-layouts: 24.1 us -> 4.11 us  [the longest x1 2.94 us: local(): return lax.switch(d, [outputs_of(dd) for dd in range(groups)], held, got)]
    squeeze x0 -> x22, local copies, waits for them, and re-layouts: none -> 13.9 us  [scatter_sum(): other = lax.dynamic_index_in_dim(x, 1 - mine, 1, keepdims=False)]
  transfers between devices with their start and end apart: 18 -> 58, of which waited for: 18 -> 29; matrix products, arithmetic and copies ran while one was open for 0% -> 5% of each run, Pallas kernels for 0% -> 0%
where the time goes in v1:
time: 825 us; the launch traced here: 816 us
  waiting for transfers between devices  424 us (51%)
  matrix products  215 us (26%)
  starting transfers between devices  105 us (13%)
  local copies, waits for them, and re-layouts  46.9 us (6%)
  other arithmetic  20.8 us (3%)
    ppermute x16, waiting for transfers between devices, shift(): return lax.ppermute(x, AXES, pairs) if pairs else jnp.zeros_like(x)  267 us
    dot_general x8, matrix products, product(): lax.dot_general(a, block, (dims, ((), ())), precision=lax.Precision.HIGH,...  215 us
    ppermute x42, waiting for transfers between devices, exchange(): return lax.ppermute(x, AXES, pairs)  157 us
    ppermute x42, starting transfers between devices, exchange(): return lax.ppermute(x, AXES, pairs)  66.6 us
    ppermute x16, starting transfers between devices, shift(): return lax.ppermute(x, AXES, pairs) if pairs else jnp.zeros_like(x)  38.5 us
    unnamed x79, local copies, waits for them, and re-layouts  17.2 us
  transfers between devices with their start and end apart: 58, of which 29 were waited for; matrix products, arithmetic and copies ran while one was open for 5% of the time, Pallas kernels for 0%

profile of v1, /device:TPU:16, one launch (start us, length us, event | category | flops | bytes accessed | tf_op | source)
XLA Modules:
  0.0 815.9 jit_solution(8075553960468280659)
XLA Ops:
  4.3 15.1 %copy.36 = f32[3,4608,256]{1,2,0:T(8,128)} copy(f32[3,4608,256]{2,1,0:T(8,128)} %param.37) | data formatting | bytes 28311552 | tf_op args[1]
  29.5 26.5 %conditional.17 = (f32[2,2,32,4608]{3,2,1,0:T(8,128)S(1)}) conditional(s32[]{:T(128)} %convert_element_type.2, (f32[128,2304]{1,0:T(8,128)S(1)}, f32[4608,2304]{1,0:T(8,128)}) %tuple.324, () %tuple.159), branch_computations={%region_4.5_spmd, %region_5.6_spmd} | conditional | flops 8153726976 | bytes 46006280 | solution.py:121
  29.7 26.3 %fusion.19 = f32[128,4608]{1,0:T(8,128)S(1)} fusion(f32[128,2304]{1,0:T(8,128)S(1)} %get-tuple-element.208, f32[4608,2304]{1,0:T(8,128)} %get-tuple-element.209), kind=kOutput, calls=%fused_computation.167 | convolution fusion | flops 8153726976 | bytes 46006272 | tf_op jit(solution)/shard_map/cond/branch_0_fun/dot_general | solution.py:79
  65.5 112.8 %collective-permute-done.13 = f32[64,2304]{1,0:T(8,128)S(1)} collective-permute-done((f32[64,2304]{1,0:T(8,128)S(1)}, f32[64,2304]{1,0:T(8,128)S(1)}, u32[]{:S(2)}, u32[]{:S(2)}) %collective-permute-start.13) | collective-permute-done | bytes 589856 | tf_op jit(solution)/shard_map/ppermute | solution.py:46
  182.1 12.0 %collective-permute-done.14 = f32[1,64,2304]{2,1,0:T(8,128)S(1)} collective-permute-done((f32[1,64,2304]{2,1,0:T(8,128)S(1)}, f32[1,64,2304]{2,1,0:T(8,128)S(1)}, u32[]{:S(2)}, u32[]{:S(2)}) %collective-permute-start.14) | collective-permute-done | bytes 589856 | tf_op jit(solution)/shard_map/ppermute | solution.py:36
  196.2 26.3 %conditional.19 = (f32[2,2,32,4608]{3,2,1,0:T(8,128)S(1)}) conditional(s32[]{:T(128)} %convert_element_type.2, (f32[128,2304]{1,0:T(8,128)S(1)}, f32[4608,2304]{1,0:T(8,128)}) %tuple.318, () %tuple.165), branch_computations={%region_8.9_spmd, %region_9.10_spmd} | conditional | flops 8153726976 | bytes 46006280 | solution.py:121
  196.2 26.3 %fusion.20 = f32[128,4608]{1,0:T(8,128)S(1)} fusion(f32[128,2304]{1,0:T(8,128)S(1)} %get-tuple-element.213, f32[4608,2304]{1,0:T(8,128)} %get-tuple-element.214), kind=kOutput, calls=%fused_computation.168 | convolution fusion | flops 8153726976 | bytes 46006272 | tf_op jit(solution)/shard_map/cond/branch_0_fun/dot_general | solution.py:79
  233.6 14.6 %collective-permute-done.17 = f32[1,32,4608]{2,1,0:T(8,128)S(1)} collective-permute-done((f32[1,32,4608]{2,1,0:T(8,128)S(1)}, f32[1,32,4608]{2,1,0:T(8,128)S(1)}, u32[]{:S(2)}, u32[]{:S(2)}) %collective-permute-start.17) | collective-permute-done | bytes 589856 | tf_op jit(solution)/shard_map/ppermute | solution.py:36
  291.7 26.5 %conditional.21 = (f32[2,2,32,4608]{3,2,1,0:T(8,128)S(1)}) conditional(s32[]{:T(128)} %convert_element_type.2, (f32[128,2304]{1,0:T(8,128)S(1)}, f32[4608,2304]{1,0:T(8,128)}) %tuple.319, () %tuple.171), branch_computations={%region_12.13_spmd, %region_13.14_spmd} | conditional | flops 8153726976 | bytes 46006280 | solution.py:121
  291.9 26.3 %fusion.21 = f32[128,4608]{1,0:T(8,128)S(1)} fusion(f32[128,2304]{1,0:T(8,128)S(1)} %get-tuple-element.218, f32[4608,2304]{1,0:T(8,128)} %get-tuple-element.219), kind=kOutput, calls=%fused_computation.169 | convolution fusion | flops 8153726976 | bytes 46006272 | tf_op jit(solution)/shard_map/cond/branch_0_fun/dot_general | solution.py:79
  329.1 14.6 %collective-permute-done.25 = f32[1,32,4608]{2,1,0:T(8,128)S(1)} collective-permute-done((f32[1,32,4608]{2,1,0:T(8,128)S(1)}, f32[1,32,4608]{2,1,0:T(8,128)S(1)}, u32[]{:S(2)}, u32[]{:S(2)}) %collective-permute-start.25) | collective-permute-done | bytes 589856 | tf_op jit(solution)/shard_map/ppermute | solution.py:36
  373.2 11.7 %collective-permute-done.30 = f32[1,64,2304]{2,1,0:T(8,128)S(1)} collective-permute-done((f32[1,64,2304]{2,1,0:T(8,128)S(1)}, f32[1,64,2304]{2,1,0:T(8,128)S(1)}, u32[]{:S(2)}, u32[]{:S(2)}) %collective-permute-start.30) | collective-permute-done | bytes 589856 | tf_op jit(solution)/shard_map/ppermute | solution.py:36
  387.1 26.3 %conditional.23 = (f32[2,2,32,4608]{3,2,1,0:T(8,128)S(1)}) conditional(s32[]{:T(128)} %convert_element_type.2, (f32[128,2304]{1,0:T(8,128)S(1)}, f32[4608,2304]{1,0:T(8,128)}) %tuple.320, () %tuple.177), branch_computations={%region_16.17_spmd, %region_17.18_spmd} | conditional | flops 8153726976 | bytes 46006280 | solution.py:121
  387.1 26.3 %fusion.22 = f32[128,4608]{1,0:T(8,128)S(1)} fusion(f32[128,2304]{1,0:T(8,128)S(1)} %get-tuple-element.223, f32[4608,2304]{1,0:T(8,128)} %get-tuple-element.224), kind=kOutput, calls=%fused_computation.170 | convolution fusion | flops 8153726976 | bytes 46006272 | tf_op jit(solution)/shard_map/cond/branch_0_fun/dot_general | solution.py:79
  424.1 14.3 %collective-permute-done.33 = f32[1,32,4608]{2,1,0:T(8,128)S(1)} collective-permute-done((f32[1,32,4608]{2,1,0:T(8,128)S(1)}, f32[1,32,4608]{2,1,0:T(8,128)S(1)}, u32[]{:S(2)}, u32[]{:S(2)}) %collective-permute-start.33) | collective-permute-done | bytes 589856 | tf_op jit(solution)/shard_map/ppermute | solution.py:36
  465.8 11.7 %collective-permute-done.38 = f32[1,64,2304]{2,1,0:T(8,128)S(1)} collective-permute-done((f32[1,64,2304]{2,1,0:T(8,128)S(1)}, f32[1,64,2304]{2,1,0:T(8,128)S(1)}, u32[]{:S(2)}, u32[]{:S(2)}) %collective-permute-start.38) | collective-permute-done | bytes 589856 | tf_op jit(solution)/shard_map/ppermute | solution.py:36
  479.6 26.5 %conditional.25 = (f32[2,2,32,4608]{3,2,1,0:T(8,128)S(1)}) conditional(s32[]{:T(128)} %convert_element_type.2, (f32[128,2304]{1,0:T(8,128)S(1)}, f32[4608,2304]{1,0:T(8,128)}) %tuple.317, () %tuple.183), branch_computations={%region_20.21_spmd, %region_21.22_spmd} | conditional | flops 8153726976 | bytes 46006280 | solution.py:121
  479.8 26.3 %fusion.23 = f32[128,4608]{1,0:T(8,128)S(1)} fusion(f32[128,2304]{1,0:T(8,128)S(1)} %get-tuple-element.228, f32[4608,2304]{1,0:T(8,128)} %get-tuple-element.229), kind=kOutput, calls=%fused_computation.171 | convolution fusion | flops 8153726976 | bytes 46006272 | tf_op jit(solution)/shard_map/cond/branch_0_fun/dot_general | solution.py:79
  517.1 14.6 %collective-permute-done.41 = f32[1,32,4608]{2,1,0:T(8,128)S(1)} collective-permute-done((f32[1,32,4608]{2,1,0:T(8,128)S(1)}, f32[1,32,4608]{2,1,0:T(8,128)S(1)}, u32[]{:S(2)}, u32[]{:S(2)}) %collective-permute-start.41) | collective-permute-done | bytes 589856 | tf_op jit(solution)/shard_map/ppermute | solution.py:36
  533.8 14.8 %collective-permute-done.43 = f32[64,2304]{1,0:T(8,128)S(1)} collective-permute-done((f32[64,2304]{1,0:T(8,128)S(1)}, f32[64,2304]{1,0:T(8,128)S(1)}, u32[]{:S(2)}, u32[]{:S(2)}) %collective-permute-start.43) | collective-permute-done | bytes 589856 | tf_op jit(solution)/shard_map/ppermute | solution.py:46
  570.8 27.9 %conditional.26 = (f32[2,2,32,4608]{3,2,1,0:T(8,128)}) conditional(s32[]{:T(128)} %convert_element_type.2, (f32[128,2304]{1,0:T(8,128)S(1)}, f32[4608,2304]{1,0:T(8,128)}) %tuple.322, () %tuple.187), branch_computations={%region_22.23_spmd, %region_23.24_spmd} | conditional | flops 8153726976 | bytes 46006280 | solution.py:121
  570.8 27.9 %fusion.24 = f32[128,4608]{1,0:T(8,128)} fusion(f32[128,2304]{1,0:T(8,128)S(1)} %get-tuple-element.230, f32[4608,2304]{1,0:T(8,128)} %get-tuple-element.231), kind=kOutput, calls=%fused_computation.172 | convolution fusion | flops 8153726976 | bytes 46006272 | tf_op jit(solution)/shard_map/cond/branch_0_fun/dot_general | solution.py:79
  608.5 13.9 %collective-permute-done.46 = f32[1,32,4608]{2,1,0:T(8,128)S(1)} collective-permute-done((f32[1,32,4608]{2,1,0:T(8,128)S(1)}, f32[1,32,4608]{2,1,0:T(8,128)S(1)}, u32[]{:S(2)}, u32[]{:S(2)}) %collective-permute-start.46) | collective-permute-done | bytes 589856 | tf_op jit(solution)/shard_map/ppermute | solution.py:36
  624.5 14.6 %collective-permute-done.48 = f32[64,2304]{1,0:T(8,128)S(1)} collective-permute-done((f32[64,2304]{1,0:T(8,128)S(1)}, f32[64,2304]{1,0:T(8,128)S(1)}, u32[]{:S(2)}, u32[]{:S(2)}) %collective-permute-start.48) | collective-permute-done | bytes 589856 | tf_op jit(solution)/shard_map/ppermute | solution.py:46
  657.4 27.9 %conditional.27 = (f32[2,2,32,4608]{3,2,1,0:T(8,128)}) conditional(s32[]{:T(128)} %convert_element_type.2, (f32[128,2304]{1,0:T(8,128)S(1)}, f32[4608,2304]{1,0:T(8,128)}) %tuple.323, () %tuple.192), branch_computations={%region_24.25_spmd, %region_25.26_spmd} | conditional | flops 8153726976 | bytes 46006280 | solution.py:121
  657.4 27.9 %fusion.25 = f32[128,4608]{1,0:T(8,128)} fusion(f32[128,2304]{1,0:T(8,128)S(1)} %get-tuple-element.232, f32[4608,2304]{1,0:T(8,128)} %get-tuple-element.233), kind=kOutput, calls=%fused_computation.173 | convolution fusion | flops 8153726976 | bytes 46006272 | tf_op jit(solution)/shard_map/cond/branch_0_fun/dot_general | solution.py:79
  694.5 14.4 %collective-permute-done.51 = f32[1,32,4608]{2,1,0:T(8,128)S(1)} collective-permute-done((f32[1,32,4608]{2,1,0:T(8,128)S(1)}, f32[1,32,4608]{2,1,0:T(8,128)S(1)}, u32[]{:S(2)}, u32[]{:S(2)}) %collective-permute-start.51) | collective-permute-done | bytes 589856 | tf_op jit(solution)/shard_map/ppermute | solution.py:36
  710.6 12.1 %collective-permute-done.53 = f32[64,2304]{1,0:T(8,128)S(1)} collective-permute-done((f32[64,2304]{1,0:T(8,128)S(1)}, f32[64,2304]{1,0:T(8,128)S(1)}, u32[]{:S(2)}, u32[]{:S(2)}) %collective-permute-start.53) | collective-permute-done | bytes 589856 | tf_op jit(solution)/shard_map/ppermute | solution.py:46
  725.5 15.6 %collective-permute-done.52 = f32[32,4608]{1,0:T(8,128)S(1)} collective-permute-done((f32[32,4608]{1,0:T(8,128)S(1)}, f32[32,4608]{1,0:T(8,128)S(1)}, u32[]{:S(2)}, u32[]{:S(2)}) %collective-permute-start.52) | collective-permute-done | bytes 589856 | tf_op jit(solution)/shard_map/ppermute | solution.py:46
  741.9 27.9 %conditional.28 = (f32[2,2,32,4608]{3,2,1,0:T(8,128)}) conditional(s32[]{:T(128)} %convert_element_type.2, (f32[128,2304]{1,0:T(8,128)S(1)}, f32[4608,2304]{1,0:T(8,128)}) %tuple.321, () %tuple.197), branch_computations={%region_26.27_spmd, %region_27.28_spmd} | conditional | flops 8153726976 | bytes 46006280 | solution.py:121
  742.0 27.7 %fusion.26 = f32[128,4608]{1,0:T(8,128)} fusion(f32[128,2304]{1,0:T(8,128)S(1)} %get-tuple-element.234, f32[4608,2304]{1,0:T(8,128)} %get-tuple-element.235), kind=kOutput, calls=%fused_computation.174 | convolution fusion | flops 8153726976 | bytes 46006272 | tf_op jit(solution)/shard_map/cond/branch_0_fun/dot_general | solution.py:79
  775.5 33.4 %collective-permute-done.57 = f32[32,4608]{1,0:T(8,128)} collective-permute-done((f32[32,4608]{1,0:T(8,128)}, f32[32,4608]{1,0:T(8,128)}, u32[]{:S(2)}, u32[]{:S(2)}) %collective-permute-start.57) | collective-permute-done | bytes 589856 | tf_op jit(solution)/shard_map/ppermute | solution.py:46
  (296 shorter events, 266.8 us)
Async XLA Ops:
  2.9 16.6 %collective-permute-start = (f32[1,32,4608]{2,1,0:T(8,128)S(1)}, f32[1,32,4608]{2,1,0:T(8,128)S(1)}, u32[]{:S(2)}, u32[]{:S(2)}) collective-permute-start(f32[1,32,4608]{2,1,0:T(8,128)S(1)} %get-tuple-element.437), channel_id=1, source_target_pairs={{0,4},{1,5},{2,6},{3,7},{4,0},{5,1},{6,2},{7,3}} | collective-permute-start | bytes 1769480 | tf_op jit(solution)/shard_map/ppermute | solution.py:36
  3.6 16.8 %collective-permute-start.3 = (f32[1,32,4608]{2,1,0:T(8,128)S(1)}, f32[1,32,4608]{2,1,0:T(8,128)S(1)}, u32[]{:S(2)}, u32[]{:S(2)}) collective-permute-start(f32[1,32,4608]{2,1,0:T(8,128)S(1)} %get-tuple-element.436), channel_id=1, source_target_pairs={{0,4},{1,5},{2,6},{3,7},{4,0},{5,1},{6,2},{7,3}} | collective-permute-start | bytes 1769480 | tf_op jit(solution)/shard_map/ppermute | solution.py:36
  63.4 114.9 %collective-permute-start.13 = (f32[64,2304]{1,0:T(8,128)S(1)}, f32[64,2304]{1,0:T(8,128)S(1)}, u32[]{:S(2)}, u32[]{:S(2)}) collective-permute-start(f32[64,2304]{1,0:T(8,128)S(1)} %fusion.4), channel_id=1, source_target_pairs={{0,8},{1,9},{2,10},{3,11},{4,12},{5,13},{6,14},{7,15},{8,16},{9,17... | collective-permute-start | bytes 1769480 | tf_op jit(solution)/shard_map/ppermute | solution.py:46
  64.8 116.3 %collective-permute-start.11 = (f32[1,32,4608]{2,1,0:T(8,128)S(1)}, f32[1,32,4608]{2,1,0:T(8,128)S(1)}, u32[]{:S(2)}, u32[]{:S(2)}) collective-permute-start(f32[1,32,4608]{2,1,0:T(8,128)S(1)} %bitcast.477), channel_id=1, source_target_pairs={{0,4},{1,5},{2,6},{3,7},{4,0},{5,1},{6,2},{7,3}} | collective-permute-start | bytes 1769480 | tf_op jit(solution)/shard_map/ppermute | solution.py:36
  178.3 15.8 %collective-permute-start.14 = (f32[1,64,2304]{2,1,0:T(8,128)S(1)}, f32[1,64,2304]{2,1,0:T(8,128)S(1)}, u32[]{:S(2)}, u32[]{:S(2)}) collective-permute-start(f32[1,64,2304]{2,1,0:T(8,128)S(1)} %bitcast.499), channel_id=1, source_target_pairs={{8,9},{9,8},{10,11},{11,10},{12,13},{13,12},{14,15},{15,14},{16,17... | collective-permute-start | bytes 1769480 | tf_op jit(solution)/shard_map/ppermute | solution.py:36
  181.3 12.9 %collective-permute-start.12 = (f32[2,32,4608]{2,1,0:T(8,128)S(1)}, f32[2,32,4608]{2,1,0:T(8,128)S(1)}, u32[]{:S(2)}, u32[]{:S(2)}) collective-permute-start(f32[2,32,4608]{2,1,0:T(8,128)S(1)} %maximum_bitcast_fusion.2), channel_id=1, source_target_pairs={{0,2},{1,3},{2,0},{3,1},{4,6},{5,7},{6,4},{7,5}} | collective-permute-start | bytes 3538952 | tf_op jit(solution)/shard_map/ppermute | solution.py:36
  230.4 17.8 %collective-permute-start.17 = (f32[1,32,4608]{2,1,0:T(8,128)S(1)}, f32[1,32,4608]{2,1,0:T(8,128)S(1)}, u32[]{:S(2)}, u32[]{:S(2)}) collective-permute-start(f32[1,32,4608]{2,1,0:T(8,128)S(1)} %constant_dynamic-slice_fusion.6), channel_id=1, source_target_pairs={{8,12},{9,13},{10,14},{11,15},{12,8},{13,9},{14,10},{15,11},{16,20... | collective-permute-start | bytes 1769480 | tf_op jit(solution)/shard_map/ppermute | solution.py:36
  248.3 15.8 %collective-permute-start.18 = (f32[32,4608]{1,0:T(8,128)S(1)}, f32[32,4608]{1,0:T(8,128)S(1)}, u32[]{:S(2)}, u32[]{:S(2)}) collective-permute-start(f32[32,4608]{1,0:T(8,128)S(1)} %bitcast_add_fusion.17), channel_id=1, source_target_pairs={{8,0},{9,1},{10,2},{11,3},{12,4},{13,5},{14,6},{15,7},{16,8},{17,9... | collective-permute-start | bytes 1769480 | tf_op jit(solution)/shard_map/ppermute | solution.py:46
  251.7 22.3 %collective-permute-start.21 = (f32[64,2304]{1,0:T(8,128)S(1)}, f32[64,2304]{1,0:T(8,128)S(1)}, u32[]{:S(2)}, u32[]{:S(2)}) collective-permute-start(f32[64,2304]{1,0:T(8,128)S(1)} %fusion.7), channel_id=1, source_target_pairs={{0,8},{1,9},{2,10},{3,11},{4,12},{5,13},{6,14},{7,15},{8,16},{9,17... | collective-permute-start | bytes 1769480 | tf_op jit(solution)/shard_map/ppermute | solution.py:46
  264.1 12.8 %collective-permute-start.19 = (f32[1,32,4608]{2,1,0:T(8,128)S(1)}, f32[1,32,4608]{2,1,0:T(8,128)S(1)}, u32[]{:S(2)}, u32[]{:S(2)}) collective-permute-start(f32[1,32,4608]{2,1,0:T(8,128)S(1)} %bitcast.478), channel_id=1, source_target_pairs={{0,4},{1,5},{2,6},{3,7},{4,0},{5,1},{6,2},{7,3}} | collective-permute-start | bytes 1769480 | tf_op jit(solution)/shard_map/ppermute | solution.py:36
  274.0 15.5 %collective-permute-start.22 = (f32[1,64,2304]{2,1,0:T(8,128)S(1)}, f32[1,64,2304]{2,1,0:T(8,128)S(1)}, u32[]{:S(2)}, u32[]{:S(2)}) collective-permute-start(f32[1,64,2304]{2,1,0:T(8,128)S(1)} %bitcast.500), channel_id=1, source_target_pairs={{8,9},{9,8},{10,11},{11,10},{12,13},{13,12},{14,15},{15,14},{16,17... | collective-permute-start | bytes 1769480 | tf_op jit(solution)/shard_map/ppermute | solution.py:36
  325.9 17.8 %collective-permute-start.25 = (f32[1,32,4608]{2,1,0:T(8,128)S(1)}, f32[1,32,4608]{2,1,0:T(8,128)S(1)}, u32[]{:S(2)}, u32[]{:S(2)}) collective-permute-start(f32[1,32,4608]{2,1,0:T(8,128)S(1)} %constant_dynamic-slice_fusion.5), channel_id=1, source_target_pairs={{8,12},{9,13},{10,14},{11,15},{12,8},{13,9},{14,10},{15,11},{16,20... | collective-permute-start | bytes 1769480 | tf_op jit(solution)/shard_map/ppermute | solution.py:36
  343.8 16.8 %collective-permute-start.26 = (f32[32,4608]{1,0:T(8,128)S(1)}, f32[32,4608]{1,0:T(8,128)S(1)}, u32[]{:S(2)}, u32[]{:S(2)}) collective-permute-start(f32[32,4608]{1,0:T(8,128)S(1)} %bitcast_add_fusion.15), channel_id=1, source_target_pairs={{8,0},{9,1},{10,2},{11,3},{12,4},{13,5},{14,6},{15,7},{16,8},{17,9... | collective-permute-start | bytes 1769480 | tf_op jit(solution)/shard_map/ppermute | solution.py:46
  347.2 22.2 %collective-permute-start.29 = (f32[64,2304]{1,0:T(8,128)S(1)}, f32[64,2304]{1,0:T(8,128)S(1)}, u32[]{:S(2)}, u32[]{:S(2)}) collective-permute-start(f32[64,2304]{1,0:T(8,128)S(1)} %fusion.10), channel_id=1, source_target_pairs={{0,8},{1,9},{2,10},{3,11},{4,12},{5,13},{6,14},{7,15},{8,16},{9,17... | collective-permute-start | bytes 1769480 | tf_op jit(solution)/shard_map/ppermute | solution.py:46
  369.4 15.5 %collective-permute-start.30 = (f32[1,64,2304]{2,1,0:T(8,128)S(1)}, f32[1,64,2304]{2,1,0:T(8,128)S(1)}, u32[]{:S(2)}, u32[]{:S(2)}) collective-permute-start(f32[1,64,2304]{2,1,0:T(8,128)S(1)} %bitcast.501), channel_id=1, source_target_pairs={{8,9},{9,8},{10,11},{11,10},{12,13},{13,12},{14,15},{15,14},{16,17... | collective-permute-start | bytes 1769480 | tf_op jit(solution)/shard_map/ppermute | solution.py:36
  372.4 12.7 %collective-permute-start.28 = (f32[2,32,4608]{2,1,0:T(8,128)S(1)}, f32[2,32,4608]{2,1,0:T(8,128)S(1)}, u32[]{:S(2)}, u32[]{:S(2)}) collective-permute-start(f32[2,32,4608]{2,1,0:T(8,128)S(1)} %maximum_bitcast_fusion.4), channel_id=1, source_target_pairs={{0,2},{1,3},{2,0},{3,1},{4,6},{5,7},{6,4},{7,5}} | collective-permute-start | bytes 3538952 | tf_op jit(solution)/shard_map/ppermute | solution.py:36
  421.0 17.4 %collective-permute-start.33 = (f32[1,32,4608]{2,1,0:T(8,128)S(1)}, f32[1,32,4608]{2,1,0:T(8,128)S(1)}, u32[]{:S(2)}, u32[]{:S(2)}) collective-permute-start(f32[1,32,4608]{2,1,0:T(8,128)S(1)} %constant_dynamic-slice_fusion.4), channel_id=1, source_target_pairs={{8,12},{9,13},{10,14},{11,15},{12,8},{13,9},{14,10},{15,11},{16,20... | collective-permute-start | bytes 1769480 | tf_op jit(solution)/shard_map/ppermute | solution.py:36
  438.5 16.4 %collective-permute-start.34 = (f32[32,4608]{1,0:T(8,128)S(1)}, f32[32,4608]{1,0:T(8,128)S(1)}, u32[]{:S(2)}, u32[]{:S(2)}) collective-permute-start(f32[32,4608]{1,0:T(8,128)S(1)} %bitcast_add_fusion.13), channel_id=1, source_target_pairs={{8,0},{9,1},{10,2},{11,3},{12,4},{13,5},{14,6},{15,7},{16,8},{17,9... | collective-permute-start | bytes 1769480 | tf_op jit(solution)/shard_map/ppermute | solution.py:46
  441.9 20.1 %collective-permute-start.37 = (f32[64,2304]{1,0:T(8,128)S(1)}, f32[64,2304]{1,0:T(8,128)S(1)}, u32[]{:S(2)}, u32[]{:S(2)}) collective-permute-start(f32[64,2304]{1,0:T(8,128)S(1)} %fusion.13), channel_id=1, source_target_pairs={{0,8},{1,9},{2,10},{3,11},{4,12},{5,13},{6,14},{7,15},{8,16},{9,17... | collective-permute-start | bytes 1769480 | tf_op jit(solution)/shard_map/ppermute | solution.py:46
  462.0 15.5 %collective-permute-start.38 = (f32[1,64,2304]{2,1,0:T(8,128)S(1)}, f32[1,64,2304]{2,1,0:T(8,128)S(1)}, u32[]{:S(2)}, u32[]{:S(2)}) collective-permute-start(f32[1,64,2304]{2,1,0:T(8,128)S(1)} %bitcast.498), channel_id=1, source_target_pairs={{8,9},{9,8},{10,11},{11,10},{12,13},{13,12},{14,15},{15,14},{16,17... | collective-permute-start | bytes 1769480 | tf_op jit(solution)/shard_map/ppermute | solution.py:36
  514.0 17.8 %collective-permute-start.41 = (f32[1,32,4608]{2,1,0:T(8,128)S(1)}, f32[1,32,4608]{2,1,0:T(8,128)S(1)}, u32[]{:S(2)}, u32[]{:S(2)}) collective-permute-start(f32[1,32,4608]{2,1,0:T(8,128)S(1)} %constant_dynamic-slice_fusion.3), channel_id=1, source_target_pairs={{8,12},{9,13},{10,14},{11,15},{12,8},{13,9},{14,10},{15,11},{16,20... | collective-permute-start | bytes 1769480 | tf_op jit(solution)/shard_map/ppermute | solution.py:36
  531.9 16.8 %collective-permute-start.43 = (f32[64,2304]{1,0:T(8,128)S(1)}, f32[64,2304]{1,0:T(8,128)S(1)}, u32[]{:S(2)}, u32[]{:S(2)}) collective-permute-start(f32[64,2304]{1,0:T(8,128)S(1)} %fusion.16), channel_id=1, source_target_pairs={{0,8},{1,9},{2,10},{3,11},{4,12},{5,13},{6,14},{7,15},{8,16},{9,17... | collective-permute-start | bytes 1769480 | tf_op jit(solution)/shard_map/ppermute | solution.py:46
  548.7 15.9 %collective-permute-start.44 = (f32[1,64,2304]{2,1,0:T(8,128)S(1)}, f32[1,64,2304]{2,1,0:T(8,128)S(1)}, u32[]{:S(2)}, u32[]{:S(2)}) collective-permute-start(f32[1,64,2304]{2,1,0:T(8,128)S(1)} %bitcast.464), channel_id=1, source_target_pairs={{8,9},{9,8},{10,11},{11,10},{12,13},{13,12},{14,15},{15,14},{16,17... | collective-permute-start | bytes 1769480 | tf_op jit(solution)/shard_map/ppermute | solution.py:36
  551.5 19.3 %collective-permute-start.42 = (f32[32,4608]{1,0:T(8,128)S(1)}, f32[32,4608]{1,0:T(8,128)S(1)}, u32[]{:S(2)}, u32[]{:S(2)}) collective-permute-start(f32[32,4608]{1,0:T(8,128)S(1)} %bitcast_add_fusion.11), channel_id=1, source_target_pairs={{8,0},{9,1},{10,2},{11,3},{12,4},{13,5},{14,6},{15,7},{16,8},{17,9... | collective-permute-start | bytes 1769480 | tf_op jit(solution)/shard_map/ppermute | solution.py:46
  605.1 17.3 %collective-permute-start.46 = (f32[1,32,4608]{2,1,0:T(8,128)S(1)}, f32[1,32,4608]{2,1,0:T(8,128)S(1)}, u32[]{:S(2)}, u32[]{:S(2)}) collective-permute-start(f32[1,32,4608]{2,1,0:T(8,128)S(1)} %constant_dynamic-slice_fusion.2), channel_id=1, source_target_pairs={{8,12},{9,13},{10,14},{11,15},{12,8},{13,9},{14,10},{15,11},{16,20... | collective-permute-start | bytes 1769480 | tf_op jit(solution)/shard_map/ppermute | solution.py:36
  622.5 16.5 %collective-permute-start.48 = (f32[64,2304]{1,0:T(8,128)S(1)}, f32[64,2304]{1,0:T(8,128)S(1)}, u32[]{:S(2)}, u32[]{:S(2)}) collective-permute-start(f32[64,2304]{1,0:T(8,128)S(1)} %collective-permute-done.43), channel_id=1, source_target_pairs={{8,16},{9,17},{10,18},{11,19},{12,20},{13,21},{14,22},{15,23},{16,... | collective-permute-start | bytes 1769480 | tf_op jit(solution)/shard_map/ppermute | solution.py:46
  639.1 15.7 %collective-permute-start.49 = (f32[1,64,2304]{2,1,0:T(8,128)S(1)}, f32[1,64,2304]{2,1,0:T(8,128)S(1)}, u32[]{:S(2)}, u32[]{:S(2)}) collective-permute-start(f32[1,64,2304]{2,1,0:T(8,128)S(1)} %bitcast.480), channel_id=1, source_target_pairs={{16,17},{17,16},{18,19},{19,18},{20,21},{21,20},{22,23},{23,22},{2... | collective-permute-start | bytes 1769480 | tf_op jit(solution)/shard_map/ppermute | solution.py:36
  642.0 15.4 %collective-permute-start.47 = (f32[32,4608]{1,0:T(8,128)S(1)}, f32[32,4608]{1,0:T(8,128)S(1)}, u32[]{:S(2)}, u32[]{:S(2)}) collective-permute-start(f32[32,4608]{1,0:T(8,128)S(1)} %bitcast_add_fusion.10), channel_id=1, source_target_pairs={{8,0},{9,1},{10,2},{11,3},{12,4},{13,5},{14,6},{15,7},{16,8},{17,9... | collective-permute-start | bytes 1769480 | tf_op jit(solution)/shard_map/ppermute | solution.py:46
  691.7 17.3 %collective-permute-start.51 = (f32[1,32,4608]{2,1,0:T(8,128)S(1)}, f32[1,32,4608]{2,1,0:T(8,128)S(1)}, u32[]{:S(2)}, u32[]{:S(2)}) collective-permute-start(f32[1,32,4608]{2,1,0:T(8,128)S(1)} %constant_dynamic-slice_fusion.1), channel_id=1, source_target_pairs={{16,20},{17,21},{18,22},{19,23},{20,16},{21,17},{22,18},{23,19},{2... | collective-permute-start | bytes 1769480 | tf_op jit(solution)/shard_map/ppermute | solution.py:36
  709.1 13.6 %collective-permute-start.53 = (f32[64,2304]{1,0:T(8,128)S(1)}, f32[64,2304]{1,0:T(8,128)S(1)}, u32[]{:S(2)}, u32[]{:S(2)}) collective-permute-start(f32[64,2304]{1,0:T(8,128)S(1)} %collective-permute-done.48), channel_id=1, source_target_pairs={{16,24},{17,25},{18,26},{19,27},{20,28},{21,29},{22,30},{23,31}} | collective-permute-start | bytes 1769480 | tf_op jit(solution)/shard_map/ppermute | solution.py:46
  723.4 17.7 %collective-permute-start.52 = (f32[32,4608]{1,0:T(8,128)S(1)}, f32[32,4608]{1,0:T(8,128)S(1)}, u32[]{:S(2)}, u32[]{:S(2)}) collective-permute-start(f32[32,4608]{1,0:T(8,128)S(1)} %bitcast_add_fusion.9), channel_id=1, source_target_pairs={{16,8},{17,9},{18,10},{19,11},{20,12},{21,13},{22,14},{23,15},{24,... | collective-permute-start | bytes 1769480 | tf_op jit(solution)/shard_map/ppermute | solution.py:46
  774.2 34.7 %collective-permute-start.57 = (f32[32,4608]{1,0:T(8,128)}, f32[32,4608]{1,0:T(8,128)}, u32[]{:S(2)}, u32[]{:S(2)}) collective-permute-start(f32[32,4608]{1,0:T(8,128)} %bitcast_add_fusion.8), channel_id=1, source_target_pairs={{24,16},{25,17},{26,18},{27,19},{28,20},{29,21},{30,22},{31,23}} | collective-permute-start | bytes 1769480 | tf_op jit(solution)/shard_map/ppermute | solution.py:46
  (66 other events, 765.0 us)

commit v2 on v1

--- a/solution.py
+++ b/solution.py
@@ -80,8 +80,8 @@
             a, block, (dims, ((), ())), precision=lax.Precision.HIGH, preferred_element_type=jnp.float32
         )
 
-    driven = excitation.transpose(0, 2, 1).reshape(STEPS, finest, CHUNKS, width, tests)
-    driven = lax.optimization_barrier(driven.transpose(0, 2, 1, 3, 4))
+    driven = lax.optimization_barrier(excitation.transpose(0, 2, 1))
+    driven = driven.reshape(STEPS, finest, CHUNKS, width, tests)
     waiting = pending[0].T.reshape(finest // rows, CHUNKS, width, tests)
     gain = sheet_gain[None, :]
     held, updated, arrived = [], [], {}
@@ -107,10 +107,13 @@
             driving = gather(future, "row", [0])
         if tail:
             whole = gather(current, "col", tail)
-        driving, whole, future, current = lax.optimization_barrier((driving, whole, future, current))
+        incident = driven[s // CHUNKS, :, s % CHUNKS].reshape(-1, tests) if driving is not None else None
+        driving, whole, future, current, incident = lax.optimization_barrier(
+            (driving, whole, future, current, incident)
+        )
         fresh, new = current, future
         if driving is not None:
-            driving = driven[s // CHUNKS, s % CHUNKS].reshape(-1, tests) - driving
+            driving = incident - driving
             part = lax.cond(
                 is_head,
                 lambda x: product(x, ((1,), (0,))),

time: 825 us -> 813 us (0.985)
  waiting for transfers between devices: 424 us -> 386 us
  other arithmetic: 20.8 us -> 32.1 us
  local copies, waits for them, and re-layouts: 46.9 us -> 57 us
    ppermute x16, waiting for transfers between devices: 267 us -> 226 us  [shift(): return lax.ppermute(x, AXES, pairs) if pairs else jnp.zeros_like(x)]
    slice x0 -> x1, local copies, waits for them, and re-layouts: none -> 9.73 us  [local(): driven[s // CHUNKS, :, s % CHUNKS].reshape(-1, tests)]
    unnamed x79 -> x89, local copies, waits for them, and re-layouts: 17.2 us -> 19.1 us
  transfers between devices with their start and end apart: 58 -> 58, of which waited for: 29 -> 32; matrix products, arithmetic and copies ran while one was open for 5% -> 6% of each run, Pallas kernels for 0% -> 0%
where the time goes in v2:
time: 813 us; the launch traced here: 804 us
  waiting for transfers between devices  386 us (47%)
  matrix products  217 us (27%)
  starting transfers between devices  108 us (13%)
  local copies, waits for them, and re-layouts  57 us (7%)
  other arithmetic  32.1 us (4%)
    ppermute x16, waiting for transfers between devices, shift(): return lax.ppermute(x, AXES, pairs) if pairs else jnp.zeros_like(x)  226 us
    dot_general x8, matrix products, product(): lax.dot_general(a, block, (dims, ((), ())), precision=lax.Precision.HIGH,...  217 us
    ppermute x42, waiting for transfers between devices, exchange(): return lax.ppermute(x, AXES, pairs)  161 us
    ppermute x42, starting transfers between devices, exchange(): return lax.ppermute(x, AXES, pairs)  71.9 us
    ppermute x16, starting transfers between devices, shift(): return lax.ppermute(x, AXES, pairs) if pairs else jnp.zeros_like(x)  35.7 us
    unnamed x89, local copies, waits for them, and re-layouts  19.1 us
  transfers between devices with their start and end apart: 58, of which 32 were waited for; matrix products, arithmetic and copies ran while one was open for 6% of the time, Pallas kernels for 0%

profile of v2, /device:TPU:16, one launch (start us, length us, event | category | flops | bytes accessed | tf_op | source)
XLA Modules:
  0.0 803.8 jit_solution(8695270279965236289)
XLA Ops:
  5.9 15.2 %copy.37 = f32[3,4608,256]{1,2,0:T(8,128)} copy(f32[3,4608,256]{2,1,0:T(8,128)} %param.37) | data formatting | bytes 28311552 | tf_op args[1]
  49.5 27.9 %conditional.17 = (f32[2,2,32,4608]{3,2,1,0:T(8,128)}) conditional(s32[]{:T(128)} %convert_element_type.2, (f32[128,2304]{1,0:T(8,128)S(1)}, f32[4608,2304]{1,0:T(8,128)}) %tuple.319, () %tuple.161), branch_computations={%region_4.5_spmd, %region_5.6_spmd} | conditional | flops 8153726976 | bytes 46006280 | solution.py:124
  49.7 27.7 %fusion.32 = f32[128,4608]{1,0:T(8,128)} fusion(f32[128,2304]{1,0:T(8,128)S(1)} %get-tuple-element.196, f32[4608,2304]{1,0:T(8,128)} %get-tuple-element.197), kind=kOutput, calls=%fused_computation.174 | convolution fusion | flops 8153726976 | bytes 46006272 | tf_op jit(solution)/shard_map/cond/branch_0_fun/dot_general | solution.py:79
  90.7 96.0 %collective-permute-done.13 = f32[64,2304]{1,0:T(8,128)S(1)} collective-permute-done((f32[64,2304]{1,0:T(8,128)}, f32[64,2304]{1,0:T(8,128)S(1)}, u32[]{:S(2)}, u32[]{:S(2)}) %collective-permute-start.13) | collective-permute-done | bytes 589856 | tf_op jit(solution)/shard_map/ppermute | solution.py:46
  190.9 11.6 %collective-permute-done.14 = f32[1,64,2304]{2,1,0:T(8,128)S(1)} collective-permute-done((f32[1,64,2304]{2,1,0:T(8,128)S(1)}, f32[1,64,2304]{2,1,0:T(8,128)S(1)}, u32[]{:S(2)}, u32[]{:S(2)}) %collective-permute-start.14) | collective-permute-done | bytes 589856 | tf_op jit(solution)/shard_map/ppermute | solution.py:36
  204.6 27.7 %conditional.19 = (f32[2,2,32,4608]{3,2,1,0:T(8,128)}) conditional(s32[]{:T(128)} %convert_element_type.2, (f32[128,2304]{1,0:T(8,128)S(1)}, f32[4608,2304]{1,0:T(8,128)}) %tuple.313, () %tuple.167), branch_computations={%region_8.9_spmd, %region_9.10_spmd} | conditional | flops 8153726976 | bytes 46006280 | solution.py:124
  204.6 27.7 %fusion.33 = f32[128,4608]{1,0:T(8,128)} fusion(f32[128,2304]{1,0:T(8,128)S(1)} %get-tuple-element.201, f32[4608,2304]{1,0:T(8,128)} %get-tuple-element.202), kind=kOutput, calls=%fused_computation.175 | convolution fusion | flops 8153726976 | bytes 46006272 | tf_op jit(solution)/shard_map/cond/branch_0_fun/dot_general | solution.py:79
  246.2 12.9 %collective-permute-done.17 = f32[1,32,4608]{2,1,0:T(8,128)S(1)} collective-permute-done((f32[1,32,4608]{2,1,0:T(8,128)S(1)}, f32[1,32,4608]{2,1,0:T(8,128)S(1)}, u32[]{:S(2)}, u32[]{:S(2)}) %collective-permute-start.17) | collective-permute-done | bytes 589856 | tf_op jit(solution)/shard_map/ppermute | solution.py:36
  283.5 11.2 %collective-permute-done.22 = f32[1,64,2304]{2,1,0:T(8,128)S(1)} collective-permute-done((f32[1,64,2304]{2,1,0:T(8,128)S(1)}, f32[1,64,2304]{2,1,0:T(8,128)S(1)}, u32[]{:S(2)}, u32[]{:S(2)}) %collective-permute-start.22) | collective-permute-done | bytes 589856 | tf_op jit(solution)/shard_map/ppermute | solution.py:36
  296.9 27.7 %conditional.21 = (f32[2,2,32,4608]{3,2,1,0:T(8,128)}) conditional(s32[]{:T(128)} %convert_element_type.2, (f32[128,2304]{1,0:T(8,128)S(1)}, f32[4608,2304]{1,0:T(8,128)}) %tuple.314, () %tuple.173), branch_computations={%region_12.13_spmd, %region_13.14_spmd} | conditional | flops 8153726976 | bytes 46006280 | solution.py:124
  296.9 27.7 %fusion.34 = f32[128,4608]{1,0:T(8,128)} fusion(f32[128,2304]{1,0:T(8,128)S(1)} %get-tuple-element.206, f32[4608,2304]{1,0:T(8,128)} %get-tuple-element.207), kind=kOutput, calls=%fused_computation.176 | convolution fusion | flops 8153726976 | bytes 46006272 | tf_op jit(solution)/shard_map/cond/branch_0_fun/dot_general | solution.py:79
  337.5 13.8 %collective-permute-done.25 = f32[1,32,4608]{2,1,0:T(8,128)S(1)} collective-permute-done((f32[1,32,4608]{2,1,0:T(8,128)S(1)}, f32[1,32,4608]{2,1,0:T(8,128)S(1)}, u32[]{:S(2)}, u32[]{:S(2)}) %collective-permute-start.25) | collective-permute-done | bytes 589856 | tf_op jit(solution)/shard_map/ppermute | solution.py:36
  385.9 27.7 %conditional.23 = (f32[2,2,32,4608]{3,2,1,0:T(8,128)}) conditional(s32[]{:T(128)} %convert_element_type.2, (f32[128,2304]{1,0:T(8,128)S(1)}, f32[4608,2304]{1,0:T(8,128)}) %tuple.315, () %tuple.179), branch_computations={%region_16.17_spmd, %region_17.18_spmd} | conditional | flops 8153726976 | bytes 46006280 | solution.py:124
  385.9 27.6 %fusion.35 = f32[128,4608]{1,0:T(8,128)} fusion(f32[128,2304]{1,0:T(8,128)S(1)} %get-tuple-element.211, f32[4608,2304]{1,0:T(8,128)} %get-tuple-element.212), kind=kOutput, calls=%fused_computation.177 | convolution fusion | flops 8153726976 | bytes 46006272 | tf_op jit(solution)/shard_map/cond/branch_0_fun/dot_general | solution.py:79
  426.4 14.0 %collective-permute-done.33 = f32[1,32,4608]{2,1,0:T(8,128)S(1)} collective-permute-done((f32[1,32,4608]{2,1,0:T(8,128)S(1)}, f32[1,32,4608]{2,1,0:T(8,128)S(1)}, u32[]{:S(2)}, u32[]{:S(2)}) %collective-permute-start.33) | collective-permute-done | bytes 589856 | tf_op jit(solution)/shard_map/ppermute | solution.py:36
  463.1 11.3 %collective-permute-done.38 = f32[1,64,2304]{2,1,0:T(8,128)S(1)} collective-permute-done((f32[1,64,2304]{2,1,0:T(8,128)S(1)}, f32[1,64,2304]{2,1,0:T(8,128)S(1)}, u32[]{:S(2)}, u32[]{:S(2)}) %collective-permute-start.38) | collective-permute-done | bytes 589856 | tf_op jit(solution)/shard_map/ppermute | solution.py:36
  475.1 28.1 %conditional.25 = (f32[2,2,32,4608]{3,2,1,0:T(8,128)}) conditional(s32[]{:T(128)} %convert_element_type.2, (f32[128,2304]{1,0:T(8,128)S(1)}, f32[4608,2304]{1,0:T(8,128)}) %tuple.312, () %tuple.185), branch_computations={%region_20.21_spmd, %region_21.22_spmd} | conditional | flops 8153726976 | bytes 46006280 | solution.py:124
  475.5 27.7 %fusion.36 = f32[128,4608]{1,0:T(8,128)} fusion(f32[128,2304]{1,0:T(8,128)S(1)} %get-tuple-element.216, f32[4608,2304]{1,0:T(8,128)} %get-tuple-element.217), kind=kOutput, calls=%fused_computation.178 | convolution fusion | flops 8153726976 | bytes 46006272 | tf_op jit(solution)/shard_map/cond/branch_0_fun/dot_general | solution.py:79
  517.1 13.1 %collective-permute-done.41 = f32[1,32,4608]{2,1,0:T(8,128)S(1)} collective-permute-done((f32[1,32,4608]{2,1,0:T(8,128)S(1)}, f32[1,32,4608]{2,1,0:T(8,128)S(1)}, u32[]{:S(2)}, u32[]{:S(2)}) %collective-permute-start.41) | collective-permute-done | bytes 589856 | tf_op jit(solution)/shard_map/ppermute | solution.py:36
  533.7 13.2 %collective-permute-done.43 = f32[64,2304]{1,0:T(8,128)S(1)} collective-permute-done((f32[64,2304]{1,0:T(8,128)S(1)}, f32[64,2304]{1,0:T(8,128)S(1)}, u32[]{:S(2)}, u32[]{:S(2)}) %collective-permute-start.43) | collective-permute-done | bytes 589856 | tf_op jit(solution)/shard_map/ppermute | solution.py:46
  566.2 26.5 %conditional.26 = (f32[2,2,32,4608]{3,2,1,0:T(8,128)S(1)}) conditional(s32[]{:T(128)} %convert_element_type.2, (f32[128,2304]{1,0:T(8,128)S(1)}, f32[4608,2304]{1,0:T(8,128)}) %tuple.317, () %tuple.189), branch_computations={%region_22.23_spmd, %region_23.24_spmd} | conditional | flops 8153726976 | bytes 46006280 | solution.py:124
  566.3 26.3 %fusion.37 = f32[128,4608]{1,0:T(8,128)S(1)} fusion(f32[128,2304]{1,0:T(8,128)S(1)} %get-tuple-element.218, f32[4608,2304]{1,0:T(8,128)} %get-tuple-element.219), kind=kOutput, calls=%fused_computation.179 | convolution fusion | flops 8153726976 | bytes 46006272 | tf_op jit(solution)/shard_map/cond/branch_0_fun/dot_general | solution.py:79
  601.3 13.8 %collective-permute-done.46 = f32[1,32,4608]{2,1,0:T(8,128)S(1)} collective-permute-done((f32[1,32,4608]{2,1,0:T(8,128)S(1)}, f32[1,32,4608]{2,1,0:T(8,128)S(1)}, u32[]{:S(2)}, u32[]{:S(2)}) %collective-permute-start.46) | collective-permute-done | bytes 589856 | tf_op jit(solution)/shard_map/ppermute | solution.py:36
  617.2 14.5 %collective-permute-done.48 = f32[64,2304]{1,0:T(8,128)S(1)} collective-permute-done((f32[64,2304]{1,0:T(8,128)S(1)}, f32[64,2304]{1,0:T(8,128)S(1)}, u32[]{:S(2)}, u32[]{:S(2)}) %collective-permute-start.48) | collective-permute-done | bytes 589856 | tf_op jit(solution)/shard_map/ppermute | solution.py:46
  650.5 26.3 %conditional.27 = (f32[2,2,32,4608]{3,2,1,0:T(8,128)S(1)}) conditional(s32[]{:T(128)} %convert_element_type.2, (f32[128,2304]{1,0:T(8,128)S(1)}, f32[4608,2304]{1,0:T(8,128)}) %tuple.318, () %tuple.194), branch_computations={%region_24.25_spmd, %region_25.26_spmd} | conditional | flops 8153726976 | bytes 46006280 | solution.py:124
  650.5 26.3 %fusion.38 = f32[128,4608]{1,0:T(8,128)S(1)} fusion(f32[128,2304]{1,0:T(8,128)S(1)} %get-tuple-element.220, f32[4608,2304]{1,0:T(8,128)} %get-tuple-element.221), kind=kOutput, calls=%fused_computation.180 | convolution fusion | flops 8153726976 | bytes 46006272 | tf_op jit(solution)/shard_map/cond/branch_0_fun/dot_general | solution.py:79
  685.1 14.2 %collective-permute-done.51 = f32[1,32,4608]{2,1,0:T(8,128)S(1)} collective-permute-done((f32[1,32,4608]{2,1,0:T(8,128)S(1)}, f32[1,32,4608]{2,1,0:T(8,128)S(1)}, u32[]{:S(2)}, u32[]{:S(2)}) %collective-permute-start.51) | collective-permute-done | bytes 589856 | tf_op jit(solution)/shard_map/ppermute | solution.py:36
  700.9 12.1 %collective-permute-done.53 = f32[64,2304]{1,0:T(8,128)S(1)} collective-permute-done((f32[64,2304]{1,0:T(8,128)S(1)}, f32[64,2304]{1,0:T(8,128)S(1)}, u32[]{:S(2)}, u32[]{:S(2)}) %collective-permute-start.53) | collective-permute-done | bytes 589856 | tf_op jit(solution)/shard_map/ppermute | solution.py:46
  715.8 15.8 %collective-permute-done.52 = f32[32,4608]{1,0:T(8,128)S(1)} collective-permute-done((f32[32,4608]{1,0:T(8,128)S(1)}, f32[32,4608]{1,0:T(8,128)S(1)}, u32[]{:S(2)}, u32[]{:S(2)}) %collective-permute-start.52) | collective-permute-done | bytes 589856 | tf_op jit(solution)/shard_map/ppermute | solution.py:46
  732.4 26.5 %conditional.28 = (f32[2,2,32,4608]{3,2,1,0:T(8,128)S(1)}) conditional(s32[]{:T(128)} %convert_element_type.2, (f32[128,2304]{1,0:T(8,128)S(1)}, f32[4608,2304]{1,0:T(8,128)}) %tuple.316, () %tuple.199), branch_computations={%region_26.27_spmd, %region_27.28_spmd} | conditional | flops 8153726976 | bytes 46006280 | solution.py:124
  732.6 26.3 %fusion.39 = f32[128,4608]{1,0:T(8,128)S(1)} fusion(f32[128,2304]{1,0:T(8,128)S(1)} %get-tuple-element.222, f32[4608,2304]{1,0:T(8,128)} %get-tuple-element.223), kind=kOutput, calls=%fused_computation.181 | convolution fusion | flops 8153726976 | bytes 46006272 | tf_op jit(solution)/shard_map/cond/branch_0_fun/dot_general | solution.py:79
  763.3 33.4 %collective-permute-done.57 = f32[32,4608]{1,0:T(8,128)} collective-permute-done((f32[32,4608]{1,0:T(8,128)}, f32[32,4608]{1,0:T(8,128)}, u32[]{:S(2)}, u32[]{:S(2)}) %collective-permute-start.57) | collective-permute-done | bytes 589856 | tf_op jit(solution)/shard_map/ppermute | solution.py:46
  (309 shorter events, 275.8 us)
Async XLA Ops:
  2.9 27.9 %collective-permute-start = (f32[1,32,4608]{2,1,0:T(8,128)S(1)}, f32[1,32,4608]{2,1,0:T(8,128)}, u32[]{:S(2)}, u32[]{:S(2)}) collective-permute-start(f32[1,32,4608]{2,1,0:T(8,128)S(1)} %get-tuple-element.409), channel_id=1, source_target_pairs={{0,4},{1,5},{2,6},{3,7},{4,0},{5,1},{6,2},{7,3}} | collective-permute-start | bytes 1769480 | tf_op jit(solution)/shard_map/ppermute | solution.py:36
  4.4 28.5 %collective-permute-start.3 = (f32[1,32,4608]{2,1,0:T(8,128)S(1)}, f32[1,32,4608]{2,1,0:T(8,128)}, u32[]{:S(2)}, u32[]{:S(2)}) collective-permute-start(f32[1,32,4608]{2,1,0:T(8,128)S(1)} %get-tuple-element.408), channel_id=1, source_target_pairs={{0,4},{1,5},{2,6},{3,7},{4,0},{5,1},{6,2},{7,3}} | collective-permute-start | bytes 1769480 | tf_op jit(solution)/shard_map/ppermute | solution.py:36
  88.6 98.1 %collective-permute-start.13 = (f32[64,2304]{1,0:T(8,128)}, f32[64,2304]{1,0:T(8,128)S(1)}, u32[]{:S(2)}, u32[]{:S(2)}) collective-permute-start(f32[64,2304]{1,0:T(8,128)} %fusion.16), channel_id=1, source_target_pairs={{0,8},{1,9},{2,10},{3,11},{4,12},{5,13},{6,14},{7,15},{8,16},{9,17... | collective-permute-start | bytes 1769480 | tf_op jit(solution)/shard_map/ppermute | solution.py:46
  90.0 99.8 %collective-permute-start.11 = (f32[1,32,4608]{2,1,0:T(8,128)S(1)}, f32[1,32,4608]{2,1,0:T(8,128)S(1)}, u32[]{:S(2)}, u32[]{:S(2)}) collective-permute-start(f32[1,32,4608]{2,1,0:T(8,128)S(1)} %bitcast.463), channel_id=1, source_target_pairs={{0,4},{1,5},{2,6},{3,7},{4,0},{5,1},{6,2},{7,3}} | collective-permute-start | bytes 1769480 | tf_op jit(solution)/shard_map/ppermute | solution.py:36
  186.7 15.8 %collective-permute-start.14 = (f32[1,64,2304]{2,1,0:T(8,128)S(1)}, f32[1,64,2304]{2,1,0:T(8,128)S(1)}, u32[]{:S(2)}, u32[]{:S(2)}) collective-permute-start(f32[1,64,2304]{2,1,0:T(8,128)S(1)} %bitcast.484), channel_id=1, source_target_pairs={{8,9},{9,8},{10,11},{11,10},{12,13},{13,12},{14,15},{15,14},{16,17... | collective-permute-start | bytes 1769480 | tf_op jit(solution)/shard_map/ppermute | solution.py:36
  190.0 12.7 %collective-permute-start.12 = (f32[2,32,4608]{2,1,0:T(8,128)S(1)}, f32[2,32,4608]{2,1,0:T(8,128)S(1)}, u32[]{:S(2)}, u32[]{:S(2)}) collective-permute-start(f32[2,32,4608]{2,1,0:T(8,128)S(1)} %maximum_bitcast_fusion.2), channel_id=1, source_target_pairs={{0,2},{1,3},{2,0},{3,1},{4,6},{5,7},{6,4},{7,5}} | collective-permute-start | bytes 3538952 | tf_op jit(solution)/shard_map/ppermute | solution.py:36
  241.7 17.4 %collective-permute-start.17 = (f32[1,32,4608]{2,1,0:T(8,128)S(1)}, f32[1,32,4608]{2,1,0:T(8,128)S(1)}, u32[]{:S(2)}, u32[]{:S(2)}) collective-permute-start(f32[1,32,4608]{2,1,0:T(8,128)S(1)} %constant_dynamic-slice_fusion.6), channel_id=1, source_target_pairs={{8,12},{9,13},{10,14},{11,15},{12,8},{13,9},{14,10},{15,11},{16,20... | collective-permute-start | bytes 1769480 | tf_op jit(solution)/shard_map/ppermute | solution.py:36
  259.2 15.4 %collective-permute-start.18 = (f32[32,4608]{1,0:T(8,128)S(1)}, f32[32,4608]{1,0:T(8,128)}, u32[]{:S(2)}, u32[]{:S(2)}) collective-permute-start(f32[32,4608]{1,0:T(8,128)S(1)} %bitcast_add_fusion.17), channel_id=1, source_target_pairs={{8,0},{9,1},{10,2},{11,3},{12,4},{13,5},{14,6},{15,7},{16,8},{17,9... | collective-permute-start | bytes 1769480 | tf_op jit(solution)/shard_map/ppermute | solution.py:46
  263.4 16.1 %collective-permute-start.21 = (f32[64,2304]{1,0:T(8,128)S(1)}, f32[64,2304]{1,0:T(8,128)S(1)}, u32[]{:S(2)}, u32[]{:S(2)}) collective-permute-start(f32[64,2304]{1,0:T(8,128)S(1)} %fusion.19), channel_id=1, source_target_pairs={{0,8},{1,9},{2,10},{3,11},{4,12},{5,13},{6,14},{7,15},{8,16},{9,17... | collective-permute-start | bytes 1769480 | tf_op jit(solution)/shard_map/ppermute | solution.py:46
  279.5 15.3 %collective-permute-start.22 = (f32[1,64,2304]{2,1,0:T(8,128)S(1)}, f32[1,64,2304]{2,1,0:T(8,128)S(1)}, u32[]{:S(2)}, u32[]{:S(2)}) collective-permute-start(f32[1,64,2304]{2,1,0:T(8,128)S(1)} %bitcast.485), channel_id=1, source_target_pairs={{8,9},{9,8},{10,11},{11,10},{12,13},{13,12},{14,15},{15,14},{16,17... | collective-permute-start | bytes 1769480 | tf_op jit(solution)/shard_map/ppermute | solution.py:36
  282.8 12.2 %collective-permute-start.20 = (f32[2,32,4608]{2,1,0:T(8,128)S(1)}, f32[2,32,4608]{2,1,0:T(8,128)S(1)}, u32[]{:S(2)}, u32[]{:S(2)}) collective-permute-start(f32[2,32,4608]{2,1,0:T(8,128)S(1)} %maximum_bitcast_fusion.3), channel_id=1, source_target_pairs={{0,2},{1,3},{2,0},{3,1},{4,6},{5,7},{6,4},{7,5}} | collective-permute-start | bytes 3538952 | tf_op jit(solution)/shard_map/ppermute | solution.py:36
  333.9 17.4 %collective-permute-start.25 = (f32[1,32,4608]{2,1,0:T(8,128)S(1)}, f32[1,32,4608]{2,1,0:T(8,128)S(1)}, u32[]{:S(2)}, u32[]{:S(2)}) collective-permute-start(f32[1,32,4608]{2,1,0:T(8,128)S(1)} %constant_dynamic-slice_fusion.5), channel_id=1, source_target_pairs={{8,12},{9,13},{10,14},{11,15},{12,8},{13,9},{14,10},{15,11},{16,20... | collective-permute-start | bytes 1769480 | tf_op jit(solution)/shard_map/ppermute | solution.py:36
  351.4 16.4 %collective-permute-start.26 = (f32[32,4608]{1,0:T(8,128)S(1)}, f32[32,4608]{1,0:T(8,128)S(1)}, u32[]{:S(2)}, u32[]{:S(2)}) collective-permute-start(f32[32,4608]{1,0:T(8,128)S(1)} %bitcast_add_fusion.15), channel_id=1, source_target_pairs={{8,0},{9,1},{10,2},{11,3},{12,4},{13,5},{14,6},{15,7},{16,8},{17,9... | collective-permute-start | bytes 1769480 | tf_op jit(solution)/shard_map/ppermute | solution.py:46
  353.8 16.1 %collective-permute-start.29 = (f32[64,2304]{1,0:T(8,128)S(1)}, f32[64,2304]{1,0:T(8,128)S(1)}, u32[]{:S(2)}, u32[]{:S(2)}) collective-permute-start(f32[64,2304]{1,0:T(8,128)S(1)} %fusion.22), channel_id=1, source_target_pairs={{0,8},{1,9},{2,10},{3,11},{4,12},{5,13},{6,14},{7,15},{8,16},{9,17... | collective-permute-start | bytes 1769480 | tf_op jit(solution)/shard_map/ppermute | solution.py:46
  369.9 15.3 %collective-permute-start.30 = (f32[1,64,2304]{2,1,0:T(8,128)S(1)}, f32[1,64,2304]{2,1,0:T(8,128)S(1)}, u32[]{:S(2)}, u32[]{:S(2)}) collective-permute-start(f32[1,64,2304]{2,1,0:T(8,128)S(1)} %bitcast.486), channel_id=1, source_target_pairs={{8,9},{9,8},{10,11},{11,10},{12,13},{13,12},{14,15},{15,14},{16,17... | collective-permute-start | bytes 1769480 | tf_op jit(solution)/shard_map/ppermute | solution.py:36
  423.0 17.4 %collective-permute-start.33 = (f32[1,32,4608]{2,1,0:T(8,128)S(1)}, f32[1,32,4608]{2,1,0:T(8,128)S(1)}, u32[]{:S(2)}, u32[]{:S(2)}) collective-permute-start(f32[1,32,4608]{2,1,0:T(8,128)S(1)} %constant_dynamic-slice_fusion.4), channel_id=1, source_target_pairs={{8,12},{9,13},{10,14},{11,15},{12,8},{13,9},{14,10},{15,11},{16,20... | collective-permute-start | bytes 1769480 | tf_op jit(solution)/shard_map/ppermute | solution.py:36
  440.5 16.4 %collective-permute-start.34 = (f32[32,4608]{1,0:T(8,128)S(1)}, f32[32,4608]{1,0:T(8,128)S(1)}, u32[]{:S(2)}, u32[]{:S(2)}) collective-permute-start(f32[32,4608]{1,0:T(8,128)S(1)} %bitcast_add_fusion.13), channel_id=1, source_target_pairs={{8,0},{9,1},{10,2},{11,3},{12,4},{13,5},{14,6},{15,7},{16,8},{17,9... | collective-permute-start | bytes 1769480 | tf_op jit(solution)/shard_map/ppermute | solution.py:46
  443.0 16.1 %collective-permute-start.37 = (f32[64,2304]{1,0:T(8,128)S(1)}, f32[64,2304]{1,0:T(8,128)S(1)}, u32[]{:S(2)}, u32[]{:S(2)}) collective-permute-start(f32[64,2304]{1,0:T(8,128)S(1)} %fusion.25), channel_id=1, source_target_pairs={{0,8},{1,9},{2,10},{3,11},{4,12},{5,13},{6,14},{7,15},{8,16},{9,17... | collective-permute-start | bytes 1769480 | tf_op jit(solution)/shard_map/ppermute | solution.py:46
  459.1 15.3 %collective-permute-start.38 = (f32[1,64,2304]{2,1,0:T(8,128)S(1)}, f32[1,64,2304]{2,1,0:T(8,128)S(1)}, u32[]{:S(2)}, u32[]{:S(2)}) collective-permute-start(f32[1,64,2304]{2,1,0:T(8,128)S(1)} %bitcast.483), channel_id=1, source_target_pairs={{8,9},{9,8},{10,11},{11,10},{12,13},{13,12},{14,15},{15,14},{16,17... | collective-permute-start | bytes 1769480 | tf_op jit(solution)/shard_map/ppermute | solution.py:36
  462.4 12.2 %collective-permute-start.36 = (f32[2,32,4608]{2,1,0:T(8,128)S(1)}, f32[2,32,4608]{2,1,0:T(8,128)S(1)}, u32[]{:S(2)}, u32[]{:S(2)}) collective-permute-start(f32[2,32,4608]{2,1,0:T(8,128)S(1)} %maximum_bitcast_fusion.5), channel_id=1, source_target_pairs={{0,2},{1,3},{2,0},{3,1},{4,6},{5,7},{6,4},{7,5}} | collective-permute-start | bytes 3538952 | tf_op jit(solution)/shard_map/ppermute | solution.py:36
  512.6 17.5 %collective-permute-start.41 = (f32[1,32,4608]{2,1,0:T(8,128)S(1)}, f32[1,32,4608]{2,1,0:T(8,128)S(1)}, u32[]{:S(2)}, u32[]{:S(2)}) collective-permute-start(f32[1,32,4608]{2,1,0:T(8,128)S(1)} %constant_dynamic-slice_fusion.3), channel_id=1, source_target_pairs={{8,12},{9,13},{10,14},{11,15},{12,8},{13,9},{14,10},{15,11},{16,20... | collective-permute-start | bytes 1769480 | tf_op jit(solution)/shard_map/ppermute | solution.py:36
  530.3 16.6 %collective-permute-start.43 = (f32[64,2304]{1,0:T(8,128)S(1)}, f32[64,2304]{1,0:T(8,128)S(1)}, u32[]{:S(2)}, u32[]{:S(2)}) collective-permute-start(f32[64,2304]{1,0:T(8,128)S(1)} %fusion.28), channel_id=1, source_target_pairs={{0,8},{1,9},{2,10},{3,11},{4,12},{5,13},{6,14},{7,15},{8,16},{9,17... | collective-permute-start | bytes 1769480 | tf_op jit(solution)/shard_map/ppermute | solution.py:46
  546.8 15.7 %collective-permute-start.44 = (f32[1,64,2304]{2,1,0:T(8,128)S(1)}, f32[1,64,2304]{2,1,0:T(8,128)S(1)}, u32[]{:S(2)}, u32[]{:S(2)}) collective-permute-start(f32[1,64,2304]{2,1,0:T(8,128)S(1)} %bitcast.450), channel_id=1, source_target_pairs={{8,9},{9,8},{10,11},{11,10},{12,13},{13,12},{14,15},{15,14},{16,17... | collective-permute-start | bytes 1769480 | tf_op jit(solution)/shard_map/ppermute | solution.py:36
  549.9 15.4 %collective-permute-start.42 = (f32[32,4608]{1,0:T(8,128)S(1)}, f32[32,4608]{1,0:T(8,128)S(1)}, u32[]{:S(2)}, u32[]{:S(2)}) collective-permute-start(f32[32,4608]{1,0:T(8,128)S(1)} %bitcast_add_fusion.11), channel_id=1, source_target_pairs={{8,0},{9,1},{10,2},{11,3},{12,4},{13,5},{14,6},{15,7},{16,8},{17,9... | collective-permute-start | bytes 1769480 | tf_op jit(solution)/shard_map/ppermute | solution.py:46
  597.7 17.4 %collective-permute-start.46 = (f32[1,32,4608]{2,1,0:T(8,128)S(1)}, f32[1,32,4608]{2,1,0:T(8,128)S(1)}, u32[]{:S(2)}, u32[]{:S(2)}) collective-permute-start(f32[1,32,4608]{2,1,0:T(8,128)S(1)} %constant_dynamic-slice_fusion.2), channel_id=1, source_target_pairs={{8,12},{9,13},{10,14},{11,15},{12,8},{13,9},{14,10},{15,11},{16,20... | collective-permute-start | bytes 1769480 | tf_op jit(solution)/shard_map/ppermute | solution.py:36
  615.2 16.4 %collective-permute-start.48 = (f32[64,2304]{1,0:T(8,128)S(1)}, f32[64,2304]{1,0:T(8,128)S(1)}, u32[]{:S(2)}, u32[]{:S(2)}) collective-permute-start(f32[64,2304]{1,0:T(8,128)S(1)} %copy-done.5), channel_id=1, source_target_pairs={{8,16},{9,17},{10,18},{11,19},{12,20},{13,21},{14,22},{15,23},{16,... | collective-permute-start | bytes 1769480 | tf_op jit(solution)/shard_map/ppermute | solution.py:46
  631.6 15.5 %collective-permute-start.49 = (f32[1,64,2304]{2,1,0:T(8,128)S(1)}, f32[1,64,2304]{2,1,0:T(8,128)S(1)}, u32[]{:S(2)}, u32[]{:S(2)}) collective-permute-start(f32[1,64,2304]{2,1,0:T(8,128)S(1)} %bitcast.466), channel_id=1, source_target_pairs={{16,17},{17,16},{18,19},{19,18},{20,21},{21,20},{22,23},{23,22},{2... | collective-permute-start | bytes 1769480 | tf_op jit(solution)/shard_map/ppermute | solution.py:36
  634.4 15.3 %collective-permute-start.47 = (f32[32,4608]{1,0:T(8,128)S(1)}, f32[32,4608]{1,0:T(8,128)S(1)}, u32[]{:S(2)}, u32[]{:S(2)}) collective-permute-start(f32[32,4608]{1,0:T(8,128)S(1)} %bitcast_add_fusion.10), channel_id=1, source_target_pairs={{8,0},{9,1},{10,2},{11,3},{12,4},{13,5},{14,6},{15,7},{16,8},{17,9... | collective-permute-start | bytes 1769480 | tf_op jit(solution)/shard_map/ppermute | solution.py:46
  681.9 17.4 %collective-permute-start.51 = (f32[1,32,4608]{2,1,0:T(8,128)S(1)}, f32[1,32,4608]{2,1,0:T(8,128)S(1)}, u32[]{:S(2)}, u32[]{:S(2)}) collective-permute-start(f32[1,32,4608]{2,1,0:T(8,128)S(1)} %constant_dynamic-slice_fusion.1), channel_id=1, source_target_pairs={{16,20},{17,21},{18,22},{19,23},{20,16},{21,17},{22,18},{23,19},{2... | collective-permute-start | bytes 1769480 | tf_op jit(solution)/shard_map/ppermute | solution.py:36
  699.4 13.6 %collective-permute-start.53 = (f32[64,2304]{1,0:T(8,128)S(1)}, f32[64,2304]{1,0:T(8,128)S(1)}, u32[]{:S(2)}, u32[]{:S(2)}) collective-permute-start(f32[64,2304]{1,0:T(8,128)S(1)} %copy-done.20), channel_id=1, source_target_pairs={{16,24},{17,25},{18,26},{19,27},{20,28},{21,29},{22,30},{23,31}} | collective-permute-start | bytes 1769480 | tf_op jit(solution)/shard_map/ppermute | solution.py:46
  713.7 17.9 %collective-permute-start.52 = (f32[32,4608]{1,0:T(8,128)S(1)}, f32[32,4608]{1,0:T(8,128)S(1)}, u32[]{:S(2)}, u32[]{:S(2)}) collective-permute-start(f32[32,4608]{1,0:T(8,128)S(1)} %bitcast_add_fusion.9), channel_id=1, source_target_pairs={{16,8},{17,9},{18,10},{19,11},{20,12},{21,13},{22,14},{23,15},{24,... | collective-permute-start | bytes 1769480 | tf_op jit(solution)/shard_map/ppermute | solution.py:46
  762.0 34.6 %collective-permute-start.57 = (f32[32,4608]{1,0:T(8,128)}, f32[32,4608]{1,0:T(8,128)}, u32[]{:S(2)}, u32[]{:S(2)}) collective-permute-start(f32[32,4608]{1,0:T(8,128)} %bitcast_add_fusion.8), channel_id=1, source_target_pairs={{24,16},{25,17},{26,18},{27,19},{28,20},{29,21},{30,22},{31,23}} | collective-permute-start | bytes 1769480 | tf_op jit(solution)/shard_map/ppermute | solution.py:46
  (72 other events, 727.2 us)

commit v3 on v2

--- a/solution.py
+++ b/solution.py
@@ -80,6 +80,11 @@
             a, block, (dims, ((), ())), precision=lax.Precision.HIGH, preferred_element_type=jnp.float32
         )
 
+    def radiate(x):
+        turned = lax.optimization_barrier(x.T)
+        field = jnp.dot(block, turned, precision=lax.Precision.HIGH, preferred_element_type=jnp.float32)
+        return lax.optimization_barrier(field).T
+
     driven = lax.optimization_barrier(excitation.transpose(0, 2, 1))
     driven = driven.reshape(STEPS, finest, CHUNKS, width, tests)
     waiting = pending[0].T.reshape(finest // rows, CHUNKS, width, tests)
@@ -124,7 +129,7 @@
             field = lax.cond(
                 is_head,
                 lambda x: jnp.zeros((x.shape[0], tests), jnp.float32),
-                lambda x: product(x, ((1,), (1,))),
+                radiate,
                 whole,
             )
         if driving is not None:

time: 813 us -> 788 us (0.969)
  matrix products: 217 us -> 170 us
  local copies, waits for them, and re-layouts: 57 us -> 85.1 us
    dot_general x8, matrix products: 217 us -> 170 us  [radiate(): jnp.dot(block, turned, precision=lax.Precision.HIGH, preferred_element_ty...]
    transpose x0 -> x8, local copies, waits for them, and re-layouts: none -> 15.9 us  [radiate(): return lax.optimization_barrier(field).T]
    unnamed x89 -> x113, local copies, waits for them, and re-layouts: 19.1 us -> 19.1 us
where the time goes in v3:
time: 788 us; the launch traced here: 779 us
  waiting for transfers between devices  389 us (49%)
  matrix products  170 us (22%)
  starting transfers between devices  105 us (13%)
  local copies, waits for them, and re-layouts  85.1 us (11%)
  other arithmetic  25.5 us (3%)
    ppermute x16, waiting for transfers between devices, shift(): return lax.ppermute(x, AXES, pairs) if pairs else jnp.zeros_like(x)  229 us
    dot_general x8, matrix products, radiate(): jnp.dot(block, turned, precision=lax.Precision.HIGH, preferred_element_ty...  170 us
    ppermute x42, waiting for transfers between devices, exchange(): return lax.ppermute(x, AXES, pairs)  160 us
    ppermute x42, starting transfers between devices, exchange(): return lax.ppermute(x, AXES, pairs)  70.1 us
    ppermute x16, starting transfers between devices, shift(): return lax.ppermute(x, AXES, pairs) if pairs else jnp.zeros_like(x)  34.9 us
    squeeze x22, local copies, waits for them, and re-layouts, scatter_sum(): other = lax.dynamic_index_in_dim(x, 1 - mine, 1, keepdims=False)  23.1 us
    unnamed x113, local copies, waits for them, and re-layouts  19.1 us
    transpose x8, local copies, waits for them, and re-layouts, radiate(): return lax.optimization_barrier(field).T  15.9 us
  transfers between devices with their start and end apart: 58, of which 32 were waited for; matrix products, arithmetic and copies ran while one was open for 6% of the time, Pallas kernels for 0%

profile of v3, /device:TPU:16, one launch (start us, length us, event | category | flops | bytes accessed | tf_op | source)
XLA Modules:
  0.0 779.3 jit_solution(10491395254587155453)
XLA Ops:
  5.9 15.1 %copy.69 = f32[3,4608,256]{1,2,0:T(8,128)} copy(f32[3,4608,256]{2,1,0:T(8,128)} %param.37) | data formatting | bytes 28311552 | tf_op args[1]
  46.4 23.7 %conditional.17 = (f32[2,2,32,4608]{3,2,1,0:T(8,128)}) conditional(s32[]{:T(128)} %convert_element_type.2, (f32[128,2304]{1,0:T(8,128)S(1)}, f32[4608,2304]{1,0:T(8,128)}) %tuple.327, () %tuple.161), branch_computations={%region_4.5_spmd, %region_5.6_spmd} | conditional | flops 8153726976 | bytes 50724872 | solution.py:129
  46.9 21.2 %fusion.32 = f32[4608,128]{1,0:T(8,128)S(1)} fusion(f32[4608,2304]{1,0:T(8,128)} %get-tuple-element.196, f32[2304,128]{0,1:T(8,128)S(1)} %bitcast.511), kind=kOutput, calls=%fused_computation.174 | convolution fusion | flops 8153726976 | bytes 46006272 | tf_op jit(solution)/shard_map/cond/branch_0_fun/dot_general | solution.py:85
  82.0 99.1 %collective-permute-done.13 = f32[64,2304]{1,0:T(8,128)S(1)} collective-permute-done((f32[64,2304]{1,0:T(8,128)S(1)}, f32[64,2304]{1,0:T(8,128)S(1)}, u32[]{:S(2)}, u32[]{:S(2)}) %collective-permute-start.13) | collective-permute-done | bytes 589856 | tf_op jit(solution)/shard_map/ppermute | solution.py:46
  185.1 11.8 %collective-permute-done.14 = f32[1,64,2304]{2,1,0:T(8,128)S(1)} collective-permute-done((f32[1,64,2304]{2,1,0:T(8,128)S(1)}, f32[1,64,2304]{2,1,0:T(8,128)S(1)}, u32[]{:S(2)}, u32[]{:S(2)}) %collective-permute-start.14) | collective-permute-done | bytes 589856 | tf_op jit(solution)/shard_map/ppermute | solution.py:36
  199.1 23.5 %conditional.19 = (f32[2,2,32,4608]{3,2,1,0:T(8,128)}) conditional(s32[]{:T(128)} %convert_element_type.2, (f32[128,2304]{1,0:T(8,128)S(1)}, f32[4608,2304]{1,0:T(8,128)}) %tuple.321, () %tuple.167), branch_computations={%region_8.9_spmd, %region_9.10_spmd} | conditional | flops 8153726976 | bytes 50724872 | solution.py:129
  199.2 21.3 %fusion.33 = f32[4608,128]{1,0:T(8,128)S(1)} fusion(f32[4608,2304]{1,0:T(8,128)} %get-tuple-element.201, f32[2304,128]{0,1:T(8,128)S(1)} %bitcast.499), kind=kOutput, calls=%fused_computation.175 | convolution fusion | flops 8153726976 | bytes 46006272 | tf_op jit(solution)/shard_map/cond/branch_0_fun/dot_general | solution.py:85
  235.1 14.2 %collective-permute-done.17 = f32[1,32,4608]{2,1,0:T(8,128)S(1)} collective-permute-done((f32[1,32,4608]{2,1,0:T(8,128)S(1)}, f32[1,32,4608]{2,1,0:T(8,128)S(1)}, u32[]{:S(2)}, u32[]{:S(2)}) %collective-permute-start.17) | collective-permute-done | bytes 589856 | tf_op jit(solution)/shard_map/ppermute | solution.py:36
  273.3 11.4 %collective-permute-done.22 = f32[1,64,2304]{2,1,0:T(8,128)S(1)} collective-permute-done((f32[1,64,2304]{2,1,0:T(8,128)S(1)}, f32[1,64,2304]{2,1,0:T(8,128)S(1)}, u32[]{:S(2)}, u32[]{:S(2)}) %collective-permute-start.22) | collective-permute-done | bytes 589856 | tf_op jit(solution)/shard_map/ppermute | solution.py:36
  286.9 23.5 %conditional.21 = (f32[2,2,32,4608]{3,2,1,0:T(8,128)}) conditional(s32[]{:T(128)} %convert_element_type.2, (f32[128,2304]{1,0:T(8,128)S(1)}, f32[4608,2304]{1,0:T(8,128)}) %tuple.322, () %tuple.173), branch_computations={%region_12.13_spmd, %region_13.14_spmd} | conditional | flops 8153726976 | bytes 50724872 | solution.py:129
  287.1 21.3 %fusion.34 = f32[4608,128]{1,0:T(8,128)S(1)} fusion(f32[4608,2304]{1,0:T(8,128)} %get-tuple-element.206, f32[2304,128]{0,1:T(8,128)S(1)} %bitcast.501), kind=kOutput, calls=%fused_computation.176 | convolution fusion | flops 8153726976 | bytes 46006272 | tf_op jit(solution)/shard_map/cond/branch_0_fun/dot_general | solution.py:85
  323.0 14.2 %collective-permute-done.25 = f32[1,32,4608]{2,1,0:T(8,128)S(1)} collective-permute-done((f32[1,32,4608]{2,1,0:T(8,128)S(1)}, f32[1,32,4608]{2,1,0:T(8,128)S(1)}, u32[]{:S(2)}, u32[]{:S(2)}) %collective-permute-start.25) | collective-permute-done | bytes 589856 | tf_op jit(solution)/shard_map/ppermute | solution.py:36
  360.2 11.5 %collective-permute-done.30 = f32[1,64,2304]{2,1,0:T(8,128)S(1)} collective-permute-done((f32[1,64,2304]{2,1,0:T(8,128)S(1)}, f32[1,64,2304]{2,1,0:T(8,128)S(1)}, u32[]{:S(2)}, u32[]{:S(2)}) %collective-permute-start.30) | collective-permute-done | bytes 589856 | tf_op jit(solution)/shard_map/ppermute | solution.py:36
  373.9 23.6 %conditional.23 = (f32[2,2,32,4608]{3,2,1,0:T(8,128)}) conditional(s32[]{:T(128)} %convert_element_type.2, (f32[128,2304]{1,0:T(8,128)S(1)}, f32[4608,2304]{1,0:T(8,128)}) %tuple.323, () %tuple.179), branch_computations={%region_16.17_spmd, %region_17.18_spmd} | conditional | flops 8153726976 | bytes 50724872 | solution.py:129
  374.3 21.2 %fusion.35 = f32[4608,128]{1,0:T(8,128)S(1)} fusion(f32[4608,2304]{1,0:T(8,128)} %get-tuple-element.211, f32[2304,128]{0,1:T(8,128)S(1)} %bitcast.503), kind=kOutput, calls=%fused_computation.177 | convolution fusion | flops 8153726976 | bytes 46006272 | tf_op jit(solution)/shard_map/cond/branch_0_fun/dot_general | solution.py:85
  410.0 14.0 %collective-permute-done.33 = f32[1,32,4608]{2,1,0:T(8,128)S(1)} collective-permute-done((f32[1,32,4608]{2,1,0:T(8,128)S(1)}, f32[1,32,4608]{2,1,0:T(8,128)S(1)}, u32[]{:S(2)}, u32[]{:S(2)}) %collective-permute-start.33) | collective-permute-done | bytes 589856 | tf_op jit(solution)/shard_map/ppermute | solution.py:36
  460.2 23.5 %conditional.25 = (f32[2,2,32,4608]{3,2,1,0:T(8,128)}) conditional(s32[]{:T(128)} %convert_element_type.2, (f32[128,2304]{1,0:T(8,128)S(1)}, f32[4608,2304]{1,0:T(8,128)}) %tuple.320, () %tuple.185), branch_computations={%region_20.21_spmd, %region_21.22_spmd} | conditional | flops 8153726976 | bytes 50724872 | solution.py:129
  460.3 21.3 %fusion.36 = f32[4608,128]{1,0:T(8,128)S(1)} fusion(f32[4608,2304]{1,0:T(8,128)} %get-tuple-element.216, f32[2304,128]{0,1:T(8,128)S(1)} %bitcast.497), kind=kOutput, calls=%fused_computation.178 | convolution fusion | flops 8153726976 | bytes 46006272 | tf_op jit(solution)/shard_map/cond/branch_0_fun/dot_general | solution.py:85
  496.2 14.2 %collective-permute-done.41 = f32[1,32,4608]{2,1,0:T(8,128)S(1)} collective-permute-done((f32[1,32,4608]{2,1,0:T(8,128)S(1)}, f32[1,32,4608]{2,1,0:T(8,128)S(1)}, u32[]{:S(2)}, u32[]{:S(2)}) %collective-permute-start.41) | collective-permute-done | bytes 589856 | tf_op jit(solution)/shard_map/ppermute | solution.py:36
  514.0 13.2 %collective-permute-done.43 = f32[64,2304]{1,0:T(8,128)S(1)} collective-permute-done((f32[64,2304]{1,0:T(8,128)S(1)}, f32[64,2304]{1,0:T(8,128)S(1)}, u32[]{:S(2)}, u32[]{:S(2)}) %collective-permute-start.43) | collective-permute-done | bytes 589856 | tf_op jit(solution)/shard_map/ppermute | solution.py:46
  546.6 23.5 %conditional.26 = (f32[2,2,32,4608]{3,2,1,0:T(8,128)}) conditional(s32[]{:T(128)} %convert_element_type.2, (f32[128,2304]{1,0:T(8,128)S(1)}, f32[4608,2304]{1,0:T(8,128)}) %tuple.325, () %tuple.189), branch_computations={%region_22.23_spmd, %region_23.24_spmd} | conditional | flops 8153726976 | bytes 50724872 | solution.py:129
  546.8 21.3 %fusion.37 = f32[4608,128]{1,0:T(8,128)S(1)} fusion(f32[4608,2304]{1,0:T(8,128)} %get-tuple-element.218, f32[2304,128]{0,1:T(8,128)S(1)} %bitcast.507), kind=kOutput, calls=%fused_computation.179 | convolution fusion | flops 8153726976 | bytes 46006272 | tf_op jit(solution)/shard_map/cond/branch_0_fun/dot_general | solution.py:85
  580.0 13.9 %collective-permute-done.46 = f32[1,32,4608]{2,1,0:T(8,128)S(1)} collective-permute-done((f32[1,32,4608]{2,1,0:T(8,128)S(1)}, f32[1,32,4608]{2,1,0:T(8,128)S(1)}, u32[]{:S(2)}, u32[]{:S(2)}) %collective-permute-start.46) | collective-permute-done | bytes 589856 | tf_op jit(solution)/shard_map/ppermute | solution.py:36
  595.9 14.5 %collective-permute-done.48 = f32[64,2304]{1,0:T(8,128)S(1)} collective-permute-done((f32[64,2304]{1,0:T(8,128)S(1)}, f32[64,2304]{1,0:T(8,128)S(1)}, u32[]{:S(2)}, u32[]{:S(2)}) %collective-permute-start.48) | collective-permute-done | bytes 589856 | tf_op jit(solution)/shard_map/ppermute | solution.py:46
  629.3 23.3 %conditional.27 = (f32[2,2,32,4608]{3,2,1,0:T(8,128)}) conditional(s32[]{:T(128)} %convert_element_type.2, (f32[128,2304]{1,0:T(8,128)S(1)}, f32[4608,2304]{1,0:T(8,128)}) %tuple.326, () %tuple.194), branch_computations={%region_24.25_spmd, %region_25.26_spmd} | conditional | flops 8153726976 | bytes 50724872 | solution.py:129
  629.3 21.3 %fusion.38 = f32[4608,128]{1,0:T(8,128)S(1)} fusion(f32[4608,2304]{1,0:T(8,128)} %get-tuple-element.220, f32[2304,128]{0,1:T(8,128)S(1)} %bitcast.509), kind=kOutput, calls=%fused_computation.180 | convolution fusion | flops 8153726976 | bytes 46006272 | tf_op jit(solution)/shard_map/cond/branch_0_fun/dot_general | solution.py:85
  662.4 14.0 %collective-permute-done.51 = f32[1,32,4608]{2,1,0:T(8,128)S(1)} collective-permute-done((f32[1,32,4608]{2,1,0:T(8,128)S(1)}, f32[1,32,4608]{2,1,0:T(8,128)S(1)}, u32[]{:S(2)}, u32[]{:S(2)}) %collective-permute-start.51) | collective-permute-done | bytes 589856 | tf_op jit(solution)/shard_map/ppermute | solution.py:36
  678.0 12.1 %collective-permute-done.53 = f32[64,2304]{1,0:T(8,128)S(1)} collective-permute-done((f32[64,2304]{1,0:T(8,128)S(1)}, f32[64,2304]{1,0:T(8,128)S(1)}, u32[]{:S(2)}, u32[]{:S(2)}) %collective-permute-start.53) | collective-permute-done | bytes 589856 | tf_op jit(solution)/shard_map/ppermute | solution.py:46
  693.0 15.8 %collective-permute-done.52 = f32[32,4608]{1,0:T(8,128)S(1)} collective-permute-done((f32[32,4608]{1,0:T(8,128)S(1)}, f32[32,4608]{1,0:T(8,128)S(1)}, u32[]{:S(2)}, u32[]{:S(2)}) %collective-permute-start.52) | collective-permute-done | bytes 589856 | tf_op jit(solution)/shard_map/ppermute | solution.py:46
  709.5 23.3 %conditional.28 = (f32[2,2,32,4608]{3,2,1,0:T(8,128)}) conditional(s32[]{:T(128)} %convert_element_type.2, (f32[128,2304]{1,0:T(8,128)S(1)}, f32[4608,2304]{1,0:T(8,128)}) %tuple.324, () %tuple.199), branch_computations={%region_26.27_spmd, %region_27.28_spmd} | conditional | flops 8153726976 | bytes 50724872 | solution.py:129
  709.5 21.3 %fusion.39 = f32[4608,128]{1,0:T(8,128)S(1)} fusion(f32[4608,2304]{1,0:T(8,128)} %get-tuple-element.222, f32[2304,128]{0,1:T(8,128)S(1)} %bitcast.505), kind=kOutput, calls=%fused_computation.181 | convolution fusion | flops 8153726976 | bytes 46006272 | tf_op jit(solution)/shard_map/cond/branch_0_fun/dot_general | solution.py:85
  738.5 33.4 %collective-permute-done.57 = f32[32,4608]{1,0:T(8,128)} collective-permute-done((f32[32,4608]{1,0:T(8,128)}, f32[32,4608]{1,0:T(8,128)}, u32[]{:S(2)}, u32[]{:S(2)}) %collective-permute-start.57) | collective-permute-done | bytes 589856 | tf_op jit(solution)/shard_map/ppermute | solution.py:46
  (341 shorter events, 292.6 us)
Async XLA Ops:
  2.9 27.9 %collective-permute-start = (f32[1,32,4608]{2,1,0:T(8,128)S(1)}, f32[1,32,4608]{2,1,0:T(8,128)}, u32[]{:S(2)}, u32[]{:S(2)}) collective-permute-start(f32[1,32,4608]{2,1,0:T(8,128)S(1)} %get-tuple-element.409), channel_id=1, source_target_pairs={{0,4},{1,5},{2,6},{3,7},{4,0},{5,1},{6,2},{7,3}} | collective-permute-start | bytes 1769480 | tf_op jit(solution)/shard_map/ppermute | solution.py:36
  4.5 28.5 %collective-permute-start.3 = (f32[1,32,4608]{2,1,0:T(8,128)S(1)}, f32[1,32,4608]{2,1,0:T(8,128)}, u32[]{:S(2)}, u32[]{:S(2)}) collective-permute-start(f32[1,32,4608]{2,1,0:T(8,128)S(1)} %get-tuple-element.408), channel_id=1, source_target_pairs={{0,4},{1,5},{2,6},{3,7},{4,0},{5,1},{6,2},{7,3}} | collective-permute-start | bytes 1769480 | tf_op jit(solution)/shard_map/ppermute | solution.py:36
  79.9 101.2 %collective-permute-start.13 = (f32[64,2304]{1,0:T(8,128)S(1)}, f32[64,2304]{1,0:T(8,128)S(1)}, u32[]{:S(2)}, u32[]{:S(2)}) collective-permute-start(f32[64,2304]{1,0:T(8,128)S(1)} %fusion.16), channel_id=1, source_target_pairs={{0,8},{1,9},{2,10},{3,11},{4,12},{5,13},{6,14},{7,15},{8,16},{9,17... | collective-permute-start | bytes 1769480 | tf_op jit(solution)/shard_map/ppermute | solution.py:46
  81.3 102.9 %collective-permute-start.11 = (f32[1,32,4608]{2,1,0:T(8,128)S(1)}, f32[1,32,4608]{2,1,0:T(8,128)S(1)}, u32[]{:S(2)}, u32[]{:S(2)}) collective-permute-start(f32[1,32,4608]{2,1,0:T(8,128)S(1)} %bitcast.479), channel_id=1, source_target_pairs={{0,4},{1,5},{2,6},{3,7},{4,0},{5,1},{6,2},{7,3}} | collective-permute-start | bytes 1769480 | tf_op jit(solution)/shard_map/ppermute | solution.py:36
  181.1 15.8 %collective-permute-start.14 = (f32[1,64,2304]{2,1,0:T(8,128)S(1)}, f32[1,64,2304]{2,1,0:T(8,128)S(1)}, u32[]{:S(2)}, u32[]{:S(2)}) collective-permute-start(f32[1,64,2304]{2,1,0:T(8,128)S(1)} %bitcast.516), channel_id=1, source_target_pairs={{8,9},{9,8},{10,11},{11,10},{12,13},{13,12},{14,15},{15,14},{16,17... | collective-permute-start | bytes 1769480 | tf_op jit(solution)/shard_map/ppermute | solution.py:36
  184.4 12.7 %collective-permute-start.12 = (f32[2,32,4608]{2,1,0:T(8,128)S(1)}, f32[2,32,4608]{2,1,0:T(8,128)S(1)}, u32[]{:S(2)}, u32[]{:S(2)}) collective-permute-start(f32[2,32,4608]{2,1,0:T(8,128)S(1)} %maximum_bitcast_fusion.2), channel_id=1, source_target_pairs={{0,2},{1,3},{2,0},{3,1},{4,6},{5,7},{6,4},{7,5}} | collective-permute-start | bytes 3538952 | tf_op jit(solution)/shard_map/ppermute | solution.py:36
  231.8 17.6 %collective-permute-start.17 = (f32[1,32,4608]{2,1,0:T(8,128)S(1)}, f32[1,32,4608]{2,1,0:T(8,128)S(1)}, u32[]{:S(2)}, u32[]{:S(2)}) collective-permute-start(f32[1,32,4608]{2,1,0:T(8,128)S(1)} %constant_dynamic-slice_fusion.6), channel_id=1, source_target_pairs={{8,12},{9,13},{10,14},{11,15},{12,8},{13,9},{14,10},{15,11},{16,20... | collective-permute-start | bytes 1769480 | tf_op jit(solution)/shard_map/ppermute | solution.py:36
  249.5 15.6 %collective-permute-start.18 = (f32[32,4608]{1,0:T(8,128)S(1)}, f32[32,4608]{1,0:T(8,128)S(1)}, u32[]{:S(2)}, u32[]{:S(2)}) collective-permute-start(f32[32,4608]{1,0:T(8,128)S(1)} %bitcast_add_fusion.17), channel_id=1, source_target_pairs={{8,0},{9,1},{10,2},{11,3},{12,4},{13,5},{14,6},{15,7},{16,8},{17,9... | collective-permute-start | bytes 1769480 | tf_op jit(solution)/shard_map/ppermute | solution.py:46
  252.9 16.3 %collective-permute-start.21 = (f32[64,2304]{1,0:T(8,128)S(1)}, f32[64,2304]{1,0:T(8,128)S(1)}, u32[]{:S(2)}, u32[]{:S(2)}) collective-permute-start(f32[64,2304]{1,0:T(8,128)S(1)} %fusion.19), channel_id=1, source_target_pairs={{0,8},{1,9},{2,10},{3,11},{4,12},{5,13},{6,14},{7,15},{8,16},{9,17... | collective-permute-start | bytes 1769480 | tf_op jit(solution)/shard_map/ppermute | solution.py:46
  269.3 15.5 %collective-permute-start.22 = (f32[1,64,2304]{2,1,0:T(8,128)S(1)}, f32[1,64,2304]{2,1,0:T(8,128)S(1)}, u32[]{:S(2)}, u32[]{:S(2)}) collective-permute-start(f32[1,64,2304]{2,1,0:T(8,128)S(1)} %bitcast.517), channel_id=1, source_target_pairs={{8,9},{9,8},{10,11},{11,10},{12,13},{13,12},{14,15},{15,14},{16,17... | collective-permute-start | bytes 1769480 | tf_op jit(solution)/shard_map/ppermute | solution.py:36
  272.5 12.4 %collective-permute-start.20 = (f32[2,32,4608]{2,1,0:T(8,128)S(1)}, f32[2,32,4608]{2,1,0:T(8,128)S(1)}, u32[]{:S(2)}, u32[]{:S(2)}) collective-permute-start(f32[2,32,4608]{2,1,0:T(8,128)S(1)} %maximum_bitcast_fusion.3), channel_id=1, source_target_pairs={{0,2},{1,3},{2,0},{3,1},{4,6},{5,7},{6,4},{7,5}} | collective-permute-start | bytes 3538952 | tf_op jit(solution)/shard_map/ppermute | solution.py:36
  319.7 17.6 %collective-permute-start.25 = (f32[1,32,4608]{2,1,0:T(8,128)S(1)}, f32[1,32,4608]{2,1,0:T(8,128)S(1)}, u32[]{:S(2)}, u32[]{:S(2)}) collective-permute-start(f32[1,32,4608]{2,1,0:T(8,128)S(1)} %constant_dynamic-slice_fusion.5), channel_id=1, source_target_pairs={{8,12},{9,13},{10,14},{11,15},{12,8},{13,9},{14,10},{15,11},{16,20... | collective-permute-start | bytes 1769480 | tf_op jit(solution)/shard_map/ppermute | solution.py:36
  337.4 16.7 %collective-permute-start.26 = (f32[32,4608]{1,0:T(8,128)S(1)}, f32[32,4608]{1,0:T(8,128)}, u32[]{:S(2)}, u32[]{:S(2)}) collective-permute-start(f32[32,4608]{1,0:T(8,128)S(1)} %bitcast_add_fusion.15), channel_id=1, source_target_pairs={{8,0},{9,1},{10,2},{11,3},{12,4},{13,5},{14,6},{15,7},{16,8},{17,9... | collective-permute-start | bytes 1769480 | tf_op jit(solution)/shard_map/ppermute | solution.py:46
  339.9 16.3 %collective-permute-start.29 = (f32[64,2304]{1,0:T(8,128)S(1)}, f32[64,2304]{1,0:T(8,128)S(1)}, u32[]{:S(2)}, u32[]{:S(2)}) collective-permute-start(f32[64,2304]{1,0:T(8,128)S(1)} %fusion.22), channel_id=1, source_target_pairs={{0,8},{1,9},{2,10},{3,11},{4,12},{5,13},{6,14},{7,15},{8,16},{9,17... | collective-permute-start | bytes 1769480 | tf_op jit(solution)/shard_map/ppermute | solution.py:46
  356.2 15.5 %collective-permute-start.30 = (f32[1,64,2304]{2,1,0:T(8,128)S(1)}, f32[1,64,2304]{2,1,0:T(8,128)S(1)}, u32[]{:S(2)}, u32[]{:S(2)}) collective-permute-start(f32[1,64,2304]{2,1,0:T(8,128)S(1)} %bitcast.518), channel_id=1, source_target_pairs={{8,9},{9,8},{10,11},{11,10},{12,13},{13,12},{14,15},{15,14},{16,17... | collective-permute-start | bytes 1769480 | tf_op jit(solution)/shard_map/ppermute | solution.py:36
  359.5 12.4 %collective-permute-start.28 = (f32[2,32,4608]{2,1,0:T(8,128)S(1)}, f32[2,32,4608]{2,1,0:T(8,128)S(1)}, u32[]{:S(2)}, u32[]{:S(2)}) collective-permute-start(f32[2,32,4608]{2,1,0:T(8,128)S(1)} %maximum_bitcast_fusion.4), channel_id=1, source_target_pairs={{0,2},{1,3},{2,0},{3,1},{4,6},{5,7},{6,4},{7,5}} | collective-permute-start | bytes 3538952 | tf_op jit(solution)/shard_map/ppermute | solution.py:36
  406.6 17.4 %collective-permute-start.33 = (f32[1,32,4608]{2,1,0:T(8,128)S(1)}, f32[1,32,4608]{2,1,0:T(8,128)S(1)}, u32[]{:S(2)}, u32[]{:S(2)}) collective-permute-start(f32[1,32,4608]{2,1,0:T(8,128)S(1)} %constant_dynamic-slice_fusion.4), channel_id=1, source_target_pairs={{8,12},{9,13},{10,14},{11,15},{12,8},{13,9},{14,10},{15,11},{16,20... | collective-permute-start | bytes 1769480 | tf_op jit(solution)/shard_map/ppermute | solution.py:36
  424.1 16.4 %collective-permute-start.34 = (f32[32,4608]{1,0:T(8,128)S(1)}, f32[32,4608]{1,0:T(8,128)S(1)}, u32[]{:S(2)}, u32[]{:S(2)}) collective-permute-start(f32[32,4608]{1,0:T(8,128)S(1)} %bitcast_add_fusion.13), channel_id=1, source_target_pairs={{8,0},{9,1},{10,2},{11,3},{12,4},{13,5},{14,6},{15,7},{16,8},{17,9... | collective-permute-start | bytes 1769480 | tf_op jit(solution)/shard_map/ppermute | solution.py:46
  426.6 16.1 %collective-permute-start.37 = (f32[64,2304]{1,0:T(8,128)S(1)}, f32[64,2304]{1,0:T(8,128)S(1)}, u32[]{:S(2)}, u32[]{:S(2)}) collective-permute-start(f32[64,2304]{1,0:T(8,128)S(1)} %fusion.25), channel_id=1, source_target_pairs={{0,8},{1,9},{2,10},{3,11},{4,12},{5,13},{6,14},{7,15},{8,16},{9,17... | collective-permute-start | bytes 1769480 | tf_op jit(solution)/shard_map/ppermute | solution.py:46
  442.7 15.3 %collective-permute-start.38 = (f32[1,64,2304]{2,1,0:T(8,128)S(1)}, f32[1,64,2304]{2,1,0:T(8,128)S(1)}, u32[]{:S(2)}, u32[]{:S(2)}) collective-permute-start(f32[1,64,2304]{2,1,0:T(8,128)S(1)} %bitcast.515), channel_id=1, source_target_pairs={{8,9},{9,8},{10,11},{11,10},{12,13},{13,12},{14,15},{15,14},{16,17... | collective-permute-start | bytes 1769480 | tf_op jit(solution)/shard_map/ppermute | solution.py:36
  492.9 17.6 %collective-permute-start.41 = (f32[1,32,4608]{2,1,0:T(8,128)S(1)}, f32[1,32,4608]{2,1,0:T(8,128)S(1)}, u32[]{:S(2)}, u32[]{:S(2)}) collective-permute-start(f32[1,32,4608]{2,1,0:T(8,128)S(1)} %constant_dynamic-slice_fusion.3), channel_id=1, source_target_pairs={{8,12},{9,13},{10,14},{11,15},{12,8},{13,9},{14,10},{15,11},{16,20... | collective-permute-start | bytes 1769480 | tf_op jit(solution)/shard_map/ppermute | solution.py:36
  510.6 16.6 %collective-permute-start.43 = (f32[64,2304]{1,0:T(8,128)S(1)}, f32[64,2304]{1,0:T(8,128)S(1)}, u32[]{:S(2)}, u32[]{:S(2)}) collective-permute-start(f32[64,2304]{1,0:T(8,128)S(1)} %fusion.28), channel_id=1, source_target_pairs={{0,8},{1,9},{2,10},{3,11},{4,12},{5,13},{6,14},{7,15},{8,16},{9,17... | collective-permute-start | bytes 1769480 | tf_op jit(solution)/shard_map/ppermute | solution.py:46
  527.2 15.7 %collective-permute-start.44 = (f32[1,64,2304]{2,1,0:T(8,128)S(1)}, f32[1,64,2304]{2,1,0:T(8,128)S(1)}, u32[]{:S(2)}, u32[]{:S(2)}) collective-permute-start(f32[1,64,2304]{2,1,0:T(8,128)S(1)} %bitcast.466), channel_id=1, source_target_pairs={{8,9},{9,8},{10,11},{11,10},{12,13},{13,12},{14,15},{15,14},{16,17... | collective-permute-start | bytes 1769480 | tf_op jit(solution)/shard_map/ppermute | solution.py:36
  530.3 15.5 %collective-permute-start.42 = (f32[32,4608]{1,0:T(8,128)S(1)}, f32[32,4608]{1,0:T(8,128)S(1)}, u32[]{:S(2)}, u32[]{:S(2)}) collective-permute-start(f32[32,4608]{1,0:T(8,128)S(1)} %bitcast_add_fusion.11), channel_id=1, source_target_pairs={{8,0},{9,1},{10,2},{11,3},{12,4},{13,5},{14,6},{15,7},{16,8},{17,9... | collective-permute-start | bytes 1769480 | tf_op jit(solution)/shard_map/ppermute | solution.py:46
  576.5 17.4 %collective-permute-start.46 = (f32[1,32,4608]{2,1,0:T(8,128)S(1)}, f32[1,32,4608]{2,1,0:T(8,128)S(1)}, u32[]{:S(2)}, u32[]{:S(2)}) collective-permute-start(f32[1,32,4608]{2,1,0:T(8,128)S(1)} %constant_dynamic-slice_fusion.2), channel_id=1, source_target_pairs={{8,12},{9,13},{10,14},{11,15},{12,8},{13,9},{14,10},{15,11},{16,20... | collective-permute-start | bytes 1769480 | tf_op jit(solution)/shard_map/ppermute | solution.py:36
  594.0 16.4 %collective-permute-start.48 = (f32[64,2304]{1,0:T(8,128)S(1)}, f32[64,2304]{1,0:T(8,128)S(1)}, u32[]{:S(2)}, u32[]{:S(2)}) collective-permute-start(f32[64,2304]{1,0:T(8,128)S(1)} %copy-done.8), channel_id=1, source_target_pairs={{8,16},{9,17},{10,18},{11,19},{12,20},{13,21},{14,22},{15,23},{16,... | collective-permute-start | bytes 1769480 | tf_op jit(solution)/shard_map/ppermute | solution.py:46
  610.4 15.5 %collective-permute-start.49 = (f32[1,64,2304]{2,1,0:T(8,128)S(1)}, f32[1,64,2304]{2,1,0:T(8,128)S(1)}, u32[]{:S(2)}, u32[]{:S(2)}) collective-permute-start(f32[1,64,2304]{2,1,0:T(8,128)S(1)} %bitcast.482), channel_id=1, source_target_pairs={{16,17},{17,16},{18,19},{19,18},{20,21},{21,20},{22,23},{23,22},{2... | collective-permute-start | bytes 1769480 | tf_op jit(solution)/shard_map/ppermute | solution.py:36
  613.2 15.3 %collective-permute-start.47 = (f32[32,4608]{1,0:T(8,128)S(1)}, f32[32,4608]{1,0:T(8,128)S(1)}, u32[]{:S(2)}, u32[]{:S(2)}) collective-permute-start(f32[32,4608]{1,0:T(8,128)S(1)} %bitcast_add_fusion.10), channel_id=1, source_target_pairs={{8,0},{9,1},{10,2},{11,3},{12,4},{13,5},{14,6},{15,7},{16,8},{17,9... | collective-permute-start | bytes 1769480 | tf_op jit(solution)/shard_map/ppermute | solution.py:46
  659.0 17.4 %collective-permute-start.51 = (f32[1,32,4608]{2,1,0:T(8,128)S(1)}, f32[1,32,4608]{2,1,0:T(8,128)S(1)}, u32[]{:S(2)}, u32[]{:S(2)}) collective-permute-start(f32[1,32,4608]{2,1,0:T(8,128)S(1)} %constant_dynamic-slice_fusion.1), channel_id=1, source_target_pairs={{16,20},{17,21},{18,22},{19,23},{20,16},{21,17},{22,18},{23,19},{2... | collective-permute-start | bytes 1769480 | tf_op jit(solution)/shard_map/ppermute | solution.py:36
  676.5 13.6 %collective-permute-start.53 = (f32[64,2304]{1,0:T(8,128)S(1)}, f32[64,2304]{1,0:T(8,128)S(1)}, u32[]{:S(2)}, u32[]{:S(2)}) collective-permute-start(f32[64,2304]{1,0:T(8,128)S(1)} %copy-done.29), channel_id=1, source_target_pairs={{16,24},{17,25},{18,26},{19,27},{20,28},{21,29},{22,30},{23,31}} | collective-permute-start | bytes 1769480 | tf_op jit(solution)/shard_map/ppermute | solution.py:46
  690.8 17.9 %collective-permute-start.52 = (f32[32,4608]{1,0:T(8,128)S(1)}, f32[32,4608]{1,0:T(8,128)S(1)}, u32[]{:S(2)}, u32[]{:S(2)}) collective-permute-start(f32[32,4608]{1,0:T(8,128)S(1)} %bitcast_add_fusion.9), channel_id=1, source_target_pairs={{16,8},{17,9},{18,10},{19,11},{20,12},{21,13},{22,14},{23,15},{24,... | collective-permute-start | bytes 1769480 | tf_op jit(solution)/shard_map/ppermute | solution.py:46
  737.2 34.6 %collective-permute-start.57 = (f32[32,4608]{1,0:T(8,128)}, f32[32,4608]{1,0:T(8,128)}, u32[]{:S(2)}, u32[]{:S(2)}) collective-permute-start(f32[32,4608]{1,0:T(8,128)} %bitcast_add_fusion.8), channel_id=1, source_target_pairs={{24,16},{25,17},{26,18},{27,19},{28,20},{29,21},{30,22},{31,23}} | collective-permute-start | bytes 1769480 | tf_op jit(solution)/shard_map/ppermute | solution.py:46
  (84 other events, 735.3 us)
